TPU v7x, 512 devices: a whole 4x8x8 slice. The times are simulated.
512 devices in a mesh: pipe: 32 (over z, y_hi, core), expert: 16 (over x, y_lo).
Axes of the slice: x: 4, y: 8 (y_hi: 2, y_lo: 4; y = y_hi * 4 + y_lo), z: 8, core: 2. Of those that a mesh axis runs over, the one named last changes fastest.
Arguments:
- fwd_in: bfloat16 [32, 1024, 3584], P('pipe', 'expert'), may hold values from -6 to 6
- bwd_in: bfloat16 [32, 1024, 3584], P('pipe', 'expert'), may hold values from -6 to 6
- bwd_grad_in: bfloat16 [32, 1024, 3584], P('pipe', 'expert'), may hold values from -6 to 6
- w_gate: bfloat16 [32, 7168, 1024], P('pipe', 'expert'), may hold values from -0.09375 to 0.09375
- w_up: bfloat16 [32, 7168, 1024], P('pipe', 'expert'), may hold values from -0.09375 to 0.09375
- w_down: bfloat16 [32, 1024, 7168], P('pipe', None, 'expert'), may hold values from -0.1875 to 0.1875
- fwd_ids: int32 [32, 1024, 1], P('pipe', 'expert'), may hold values from 0 to 1; in each aligned block of 64 rows (0 to 63, 64 to 127, ..., all dimensions but the last counted through in order) at most 40 rows name the same one
- fwd_gates: float32 [32, 1024, 1], P('pipe', 'expert'), may hold values from 0.25 to 1
- bwd_ids: int32 [32, 1024, 1], P('pipe', 'expert'), may hold values from 0 to 1; in each aligned block of 64 rows (0 to 63, 64 to 127, ..., all dimensions but the last counted through in order) at most 40 rows name the same one
- bwd_gates: float32 [32, 1024, 1], P('pipe', 'expert'), may hold values from 0.25 to 1
Outputs:
- fwd_out: bfloat16 [32, 1024, 3584], P('pipe', 'expert')
- bwd_out: bfloat16 [32, 1024, 3584], P('pipe', 'expert')
Inputs may be any that keep to these rules, and one draw needn't show every extreme that they name: `fwd_ids`: each row names 1 different experts; among the 64 tokens of one device (aligned blocks of rows) no expert is named more than 40 times. `bwd_ids`: each row names 1 different experts; among the 64 tokens of one device (aligned blocks of rows) no expert is named more than 40 times.
All inputs are finite; a program needn't handle non-finite values.
Results may differ from a plain program's by a relative error of at most 0.01.
Values may be sent and summed in bfloat16 or wider, within the bound.
A program may use at most 128 MiB of HBM per device.

v0:
```python
import jax
import jax.numpy as jnp
from jax import lax
from jax.sharding import PartitionSpec as P

EXPERTS = 2
TOP = 1
CAP = 40


def partner(value, axis, bit):
    mask = 2**bit
    pairs = [(source, source ^ mask) for source in range(lax.axis_size(axis))]
    return lax.ppermute(value, axis, pairs)


def shifted(x, axis, by):
    length = lax.axis_size(axis)
    pairs = [(i, i + by) for i in range(length) if 0 <= i + by < length]
    return lax.ppermute(x, axis, pairs)


def slot_positions(expert_ids):
    flat_ids = expert_ids.reshape(-1)
    onehot = (flat_ids[:, None] == jnp.arange(EXPERTS, dtype=jnp.int32)[None, :]).astype(jnp.int32)
    before = jnp.cumsum(onehot, axis=0) - onehot
    slot_pos = jnp.sum(before * onehot, axis=1)
    return flat_ids * CAP + slot_pos


def dispatch_rows(inputs, position, group):
    token_count, model_width = inputs.shape
    slots_total = EXPERTS * CAP
    match = (jnp.arange(slots_total, dtype=jnp.int32)[:, None] == position[None, :]).astype(
        jnp.int32
    )
    table = jnp.sum(match.reshape(slots_total, token_count, TOP), axis=2).astype(jnp.bfloat16)
    table = table.reshape(EXPERTS, CAP, token_count)
    pieces = inputs.reshape(token_count, group, model_width // group)
    filled = jnp.einsum("ect,tgk->egck", table, pieces, preferred_element_type=jnp.float32).astype(
        jnp.bfloat16
    )
    return filled.reshape(EXPERTS * group, CAP, model_width // group)


def combine_rows(residual, returned, expert_ids, position, gate_values, group):
    token_count, model_width = residual.shape
    blocks = returned.reshape(EXPERTS, group, CAP, model_width // group)
    flat_ids = expert_ids.reshape(-1)
    slot_pos = position - flat_ids * CAP
    picked = blocks[flat_ids, :, slot_pos, :].reshape(token_count, TOP, model_width)
    summed = jnp.sum(gate_values[:, :, None] * picked.astype(jnp.float32), axis=1)
    return (residual.astype(jnp.float32) + summed).astype(jnp.bfloat16)


def group_reduce(partial_value, bits, my_index):
    current = partial_value
    for bit in range(bits):
        half = current.shape[0] // 2
        my_bit = my_index >> bit & 1
        keep = jnp.where(my_bit == 0, current[:half], current[half:])
        given = jnp.where(my_bit == 0, current[half:], current[:half])
        got = partner(given.astype(jnp.bfloat16), "expert", bit)
        current = keep + got.astype(jnp.float32)
    return current


def group_collect(block, bits, my_index):
    current = block
    for bit in reversed(range(bits)):
        got = partner(current, "expert", bit)
        my_bit = my_index >> bit & 1
        current = jnp.where(
            my_bit == 0,
            jnp.concatenate([current, got], axis=0),
            jnp.concatenate([got, current], axis=0),
        )
    return current


def hidden_of(summed, hidden_units):
    return (jax.nn.silu(summed[:, :hidden_units]) * summed[:, hidden_units:]).astype(jnp.bfloat16)


def grads_of(summed, hidden_units):
    back_gate = summed[:, :hidden_units]
    back_up = summed[:, hidden_units : 2 * hidden_units]
    grad_hidden = summed[:, 2 * hidden_units :]
    sig_gate = jax.nn.sigmoid(back_gate)
    grad_gate = (grad_hidden * back_up * sig_gate * (1.0 + back_gate * (1.0 - sig_gate))).astype(
        jnp.bfloat16
    )
    grad_up = (grad_hidden * (back_gate * sig_gate)).astype(jnp.bfloat16)
    return jnp.concatenate([grad_gate, grad_up], axis=1)


def body(fwd_in, bwd_in, bwd_grad_in, w_gate, w_up, w_down, fwd_ids, fwd_gates, bwd_ids, bwd_gates):
    section_index = lax.axis_index("pipe")
    final_section = lax.axis_size("pipe") - 1
    group = lax.axis_size("expert") // EXPERTS
    bits = group.bit_length() - 1
    my_index = lax.axis_index("expert")
    arrived = shifted(fwd_in, "pipe", 1)
    section_x = jnp.where(section_index == 0, fwd_in, arrived)[0]
    came_back = shifted(bwd_grad_in, "pipe", -1)
    section_g = jnp.where(section_index == final_section, bwd_grad_in, came_back)[0]
    saved_x = bwd_in[0]
    in_mats = jnp.concatenate([w_gate[0], w_up[0]], axis=1)
    down_mats = w_down[0]
    hidden_units = down_mats.shape[0]
    fwd_position = slot_positions(fwd_ids[0])
    bwd_position = slot_positions(bwd_ids[0])
    send_fwd = dispatch_rows(section_x, fwd_position, group)
    send_saved = dispatch_rows(saved_x, bwd_position, group)
    send_grad = dispatch_rows(section_g, bwd_position, group)
    received = lax.all_to_all(send_fwd, "expert", split_axis=0, concat_axis=0, tiled=True)
    source_count, slot_count, width = received.shape
    rows = received.reshape(source_count * slot_count, width)
    partial_value = jnp.dot(rows, in_mats, preferred_element_type=jnp.float32)
    block = group_reduce(partial_value, bits, my_index)
    hidden = group_collect(hidden_of(block, hidden_units), bits, my_index)
    produced = jnp.dot(hidden, down_mats, preferred_element_type=jnp.float32).astype(jnp.bfloat16)
    back_fwd = lax.all_to_all(
        produced.reshape(source_count, slot_count, width),
        "expert",
        split_axis=0,
        concat_axis=0,
        tiled=True,
    )
    received = lax.all_to_all(send_saved, "expert", split_axis=0, concat_axis=0, tiled=True)
    source_count, slot_count, width = received.shape
    rows = received.reshape(source_count * slot_count, width)
    grad_rows = lax.all_to_all(
        send_grad, "expert", split_axis=0, concat_axis=0, tiled=True
    ).reshape(source_count * slot_count, width)
    partial_value = jnp.concatenate(
        [
            jnp.dot(rows, in_mats, preferred_element_type=jnp.float32),
            jnp.dot(grad_rows, down_mats.T, preferred_element_type=jnp.float32),
        ],
        axis=1,
    )
    block = group_reduce(partial_value, bits, my_index)
    joined = group_collect(grads_of(block, hidden_units), bits, my_index)
    produced = jnp.dot(joined, in_mats.T, preferred_element_type=jnp.float32).astype(jnp.bfloat16)
    back_bwd = lax.all_to_all(
        produced.reshape(source_count, slot_count, width),
        "expert",
        split_axis=0,
        concat_axis=0,
        tiled=True,
    )
    fwd_out = combine_rows(section_x, back_fwd, fwd_ids[0], fwd_position, fwd_gates[0], group)
    bwd_out = combine_rows(section_g, back_bwd, bwd_ids[0], bwd_position, bwd_gates[0], group)
    return (fwd_out[None], bwd_out[None])


def solution(mesh):
    return jax.shard_map(
        body,
        mesh=mesh,
        in_specs=(
            P("pipe", "expert", None),
            P("pipe", "expert", None),
            P("pipe", "expert", None),
            P("pipe", "expert", None),
            P("pipe", "expert", None),
            P("pipe", None, "expert"),
            P("pipe", "expert", None),
            P("pipe", "expert", None),
            P("pipe", "expert", None),
            P("pipe", "expert", None),
        ),
        out_specs=(P("pipe", "expert", None), P("pipe", "expert", None)),
        check_vma=False,
    )
```

profile of v0, /device:TPU:250, one launch (start us, length us, event | category | flops | bytes accessed | tf_op | source)
XLA Modules:
  0.0 363.7 jit_solution(7475344604437741651)
XLA Ops:
  6.0 7.6 %all-to-all-start.2 = ((bf16[16,40,448]{2,1,0:T(8,128)(2,1)}), bf16[16,40,448]{2,1,0:T(8,128)(2,1)S(1)}, u32[]{:S(2)}, u32[]{:S(2)}) async-start(bf16[16,40,448]{2,1,0:T(8,128)(2,1)} %bitcast.21), calls=%async_computation.2 | async-start | bytes 1310720 | tf_op jit(solution)/shard_map/all_to_all | solution.py:130
  13.6 3.6 collective-permute-start.7
  19.5 24.2 %collective-permute-done.7 = bf16[1,64,3584]{2,1,0:T(8,128)(2,1)} collective-permute-done((bf16[1,64,3584]{2,1,0:T(8,128)(2,1)S(1)}, bf16[1,64,3584]{2,1,0:T(8,128)(2,1)}, u32[]{:S(2)}, u32[]{:S(2)}) %collective-permute-start.7) | collective-permute-done | bytes 458784 | tf_op jit(solution)/shard_map/ppermute | solution.py:20
  48.2 7.9 %all-to-all-start.3 = ((bf16[16,40,448]{2,1,0:T(8,128)(2,1)}), bf16[16,40,448]{2,1,0:T(8,128)(2,1)S(1)}, u32[]{:S(2)}, u32[]{:S(2)}) async-start(bf16[16,40,448]{2,1,0:T(8,128)(2,1)} %bitcast.25), calls=%async_computation.3 | async-start | bytes 1310720 | tf_op jit(solution)/shard_map/all_to_all | solution.py:133
  59.4 3.9 %fusion.20 = f32[640,2048]{1,0:T(8,128)} fusion(bf16[640,448]{1,0:T(8,128)(2,1)S(1)} %bitcast.74, bf16[448,1024]{1,0:T(8,128)(2,1)S(1)} %bitcast.83, bf16[448,1024]{1,0:T(8,128)(2,1)S(1)} %bitcast.86), kind=kOutput, calls=%fused_computation.49 | convolution fusion | flops 1178075136 | bytes 7651328 | tf_op jit(solution)/shard_map/dot_general | solution.py:138
  63.3 8.3 %all-to-all-done.3 = bf16[16,40,448]{2,1,0:T(8,128)(2,1)S(1)} async-done(((bf16[16,40,448]{2,1,0:T(8,128)(2,1)}), bf16[16,40,448]{2,1,0:T(8,128)(2,1)S(1)}, u32[]{:S(2)}, u32[]{:S(2)}) %all-to-all-start.3) | async-done | bytes 573472 | tf_op jit(solution)/shard_map/all_to_all | solution.py:133
  71.5 8.1 %all-to-all-start = ((bf16[16,40,448]{2,1,0:T(8,128)(2,1)}), bf16[16,40,448]{2,1,0:T(8,128)(2,1)}, u32[]{:S(2)}, u32[]{:S(2)}) async-start(bf16[16,40,448]{2,1,0:T(8,128)(2,1)} %bitcast.5), calls=%async_computation | async-start | bytes 1310720 | tf_op jit(solution)/shard_map/all_to_all | solution.py:116
  79.7 2.1 fusion.17
  83.9 2.5 collective-permute-start.8
  86.4 9.8 %all-to-all-done = bf16[16,40,448]{2,1,0:T(8,128)(2,1)} async-done(((bf16[16,40,448]{2,1,0:T(8,128)(2,1)}), bf16[16,40,448]{2,1,0:T(8,128)(2,1)}, u32[]{:S(2)}, u32[]{:S(2)}) %all-to-all-start) | async-done | bytes 573472 | tf_op jit(solution)/shard_map/all_to_all | solution.py:116
  96.2 3.3 fusion.21
  99.8 3.1 collective-permute-start.1
  102.9 31.7 %collective-permute-done.8 = bf16[320,3072]{1,0:T(8,128)(2,1)} collective-permute-done((bf16[320,3072]{1,0:T(8,128)(2,1)}, bf16[320,3072]{1,0:T(8,128)(2,1)}, u32[]{:S(2)}, u32[]{:S(2)}) %collective-permute-start.8) | collective-permute-done | bytes 1966112 | tf_op jit(solution)/shard_map/ppermute | solution.py:14
  136.8 2.5 collective-permute-start.9
  139.3 43.6 %collective-permute-done.1 = bf16[320,2048]{1,0:T(8,128)(2,1)S(1)} collective-permute-done((bf16[320,2048]{1,0:T(8,128)(2,1)S(1)}, bf16[320,2048]{1,0:T(8,128)(2,1)S(1)}, u32[]{:S(2)}, u32[]{:S(2)}) %collective-permute-start.1) | collective-permute-done | bytes 1310752 | tf_op jit(solution)/shard_map/ppermute | solution.py:14
  183.9 2.3 collective-permute-start.2
  186.7 2.4 collective-permute-start.10
  189.1 28.1 %collective-permute-done.2 = bf16[160,2048]{1,0:T(8,128)(2,1)S(1)} collective-permute-done((bf16[160,2048]{1,0:T(8,128)(2,1)S(1)}, bf16[160,2048]{1,0:T(8,128)(2,1)S(1)}, u32[]{:S(2)}, u32[]{:S(2)}) %collective-permute-start.2) | collective-permute-done | bytes 655392 | tf_op jit(solution)/shard_map/ppermute | solution.py:14
  217.5 2.4 collective-permute-start.3
  220.4 3.4 collective-permute-start.11
  223.8 6.2 %collective-permute-done.3 = bf16[80,2048]{1,0:T(8,128)(2,1)S(1)} collective-permute-done((bf16[80,2048]{1,0:T(8,128)(2,1)S(1)}, bf16[80,2048]{1,0:T(8,128)(2,1)S(1)}, u32[]{:S(2)}, u32[]{:S(2)}) %collective-permute-start.3) | collective-permute-done | bytes 327712 | tf_op jit(solution)/shard_map/ppermute | solution.py:14
  230.2 2.4 collective-permute-start.4
  232.6 4.4 %collective-permute-done.11 = bf16[80,2048]{1,0:T(8,128)(2,1)S(1)} collective-permute-done((bf16[80,2048]{1,0:T(8,128)(2,1)S(1)}, bf16[80,2048]{1,0:T(8,128)(2,1)S(1)}, u32[]{:S(2)}, u32[]{:S(2)}) %collective-permute-start.11) | collective-permute-done | bytes 327712 | tf_op jit(solution)/shard_map/ppermute | solution.py:14
  239.7 4.5 %collective-permute-start.5 = (bf16[160,1024]{1,0:T(8,128)(2,1)S(1)}, bf16[160,1024]{1,0:T(8,128)(2,1)S(1)}, u32[]{:S(2)}, u32[]{:S(2)}) collective-permute-start(bf16[160,1024]{1,0:T(8,128)(2,1)S(1)} %maximum_select_fusion.9), channel_id=1, source_target_pairs={{0,2},{1,3},{2,0},{3,1},{4,6},{5,7},{6,4},{7,5},{8,10},{9,11},{10,... | collective-permute-start | bytes 983048 | tf_op jit(solution)/shard_map/ppermute | solution.py:14
  244.2 37.8 %collective-permute-done.5 = bf16[160,1024]{1,0:T(8,128)(2,1)S(1)} collective-permute-done((bf16[160,1024]{1,0:T(8,128)(2,1)S(1)}, bf16[160,1024]{1,0:T(8,128)(2,1)S(1)}, u32[]{:S(2)}, u32[]{:S(2)}) %collective-permute-start.5) | collective-permute-done | bytes 327712 | tf_op jit(solution)/shard_map/ppermute | solution.py:14
  285.6 3.9 %collective-permute-start.13 = (bf16[320,2048]{1,0:T(8,128)(2,1)}, bf16[320,2048]{1,0:T(8,128)(2,1)}, u32[]{:S(2)}, u32[]{:S(2)}) collective-permute-start(bf16[320,2048]{1,0:T(8,128)(2,1)} %maximum_select_fusion.6), channel_id=1, source_target_pairs={{0,1},{1,0},{2,3},{3,2},{4,5},{5,4},{6,7},{7,6},{8,9},{9,8},{10,11... | collective-permute-start | bytes 3932168 | tf_op jit(solution)/shard_map/ppermute | solution.py:14
  289.5 12.1 %collective-permute-done.6 = bf16[320,1024]{1,0:T(8,128)(2,1)S(1)} collective-permute-done((bf16[320,1024]{1,0:T(8,128)(2,1)S(1)}, bf16[320,1024]{1,0:T(8,128)(2,1)S(1)}, u32[]{:S(2)}, u32[]{:S(2)}) %collective-permute-start.6) | collective-permute-done | bytes 655392 | tf_op jit(solution)/shard_map/ppermute | solution.py:14
  303.7 7.5 %all-to-all-start.1 = ((bf16[16,40,448]{2,1,0:T(8,128)(2,1)}), bf16[16,40,448]{2,1,0:T(8,128)(2,1)S(1)}, u32[]{:S(2)}, u32[]{:S(2)}) async-start(bf16[16,40,448]{2,1,0:T(8,128)(2,1)} %bitcast.10), calls=%async_computation.1 | async-start | bytes 1310720 | tf_op jit(solution)/shard_map/all_to_all | solution.py:123
  311.3 22.7 %collective-permute-done.13 = bf16[320,2048]{1,0:T(8,128)(2,1)} collective-permute-done((bf16[320,2048]{1,0:T(8,128)(2,1)}, bf16[320,2048]{1,0:T(8,128)(2,1)}, u32[]{:S(2)}, u32[]{:S(2)}) %collective-permute-start.13) | collective-permute-done | bytes 1310752 | tf_op jit(solution)/shard_map/ppermute | solution.py:14
  334.0 4.8 %fusion.8 = bf16[640,448]{0,1:T(8,128)(2,1)S(1)} fusion(bf16[320,2048]{1,0:T(8,128)(2,1)} %collective-permute-done.13, bf16[320,2048]{1,0:T(8,128)(2,1)} %maximum_select_fusion.6, pred[]{:T(512)S(6)} %eq.128, bf16[448,1024]{1,0:T(8,128)(2,1)} %bitcast.82, bf16[448,1024]{1,0:T(8,128)(2,1)} %bitcast.85), kind=kOutput, calls=%fused_computation.24 | convolution fusion | flops 1190158336 | bytes 5029889 | tf_op jit(solution)/shard_map/dot_general | solution.py:145
  340.6 7.3 %all-to-all-start.4 = ((bf16[16,40,448]{2,1,0:T(8,128)(2,1)}), bf16[16,40,448]{2,1,0:T(8,128)(2,1)S(1)}, u32[]{:S(2)}, u32[]{:S(2)}) async-start(bf16[16,40,448]{2,1,0:T(8,128)(2,1)} %bitcast.27), calls=%async_computation.4 | async-start | bytes 1310720 | tf_op jit(solution)/shard_map/all_to_all | solution.py:146
  352.3 9.1 %all-to-all-done.4 = bf16[16,40,448]{2,1,0:T(8,128)(2,1)S(1)} async-done(((bf16[16,40,448]{2,1,0:T(8,128)(2,1)}), bf16[16,40,448]{2,1,0:T(8,128)(2,1)S(1)}, u32[]{:S(2)}, u32[]{:S(2)}) %all-to-all-start.4) | async-done | bytes 573472 | tf_op jit(solution)/shard_map/all_to_all | solution.py:146
  (96 shorter events, 39.0 us)
Async XLA Ops:
  0.6 79.0 %copy-start = (bf16[1,1024,448]{1,2,0:T(8,128)(2,1)S(1)}, bf16[1,1024,448]{1,2,0:T(8,128)(2,1)}, u32[]{:S(2)}) copy-start(bf16[1,1024,448]{1,2,0:T(8,128)(2,1)} %param.15) | copy-start | bytes 2752516
  0.6 12.9 %copy-start.7 = (bf16[1,64,3584]{2,1,0:T(8,128)(2,1)S(1)}, bf16[1,64,3584]{2,1,0:T(8,128)(2,1)}, u32[]{:S(2)}) copy-start(bf16[1,64,3584]{2,1,0:T(8,128)(2,1)} %param.12) | copy-start | bytes 1376260
  0.7 16.5 %copy-start.8 = (bf16[1,64,3584]{2,1,0:T(8,128)(2,1)S(1)}, bf16[1,64,3584]{2,1,0:T(8,128)(2,1)}, u32[]{:S(2)}) copy-start(bf16[1,64,3584]{2,1,0:T(8,128)(2,1)} %param.10) | copy-start | bytes 1376260
  0.7 18.4 %copy-start.10 = (s32[1,64,1]{1,2,0:T(1,128)S(1)}, s32[1,64,1]{1,2,0:T(1,128)}, u32[]{:S(2)}) copy-start(s32[1,64,1]{1,2,0:T(1,128)} %param.16) | copy-start | bytes 772
  6.0 42.2 %all-to-all-start.2 = ((bf16[16,40,448]{2,1,0:T(8,128)(2,1)}), bf16[16,40,448]{2,1,0:T(8,128)(2,1)S(1)}, u32[]{:S(2)}, u32[]{:S(2)}) async-start(bf16[16,40,448]{2,1,0:T(8,128)(2,1)} %bitcast.21), calls=%async_computation.2 | async-start | bytes 1310720 | tf_op jit(solution)/shard_map/all_to_all | solution.py:130
  13.6 30.1 %collective-permute-start.7 = (bf16[1,64,3584]{2,1,0:T(8,128)(2,1)S(1)}, bf16[1,64,3584]{2,1,0:T(8,128)(2,1)}, u32[]{:S(2)}, u32[]{:S(2)}) collective-permute-start(bf16[1,64,3584]{2,1,0:T(8,128)(2,1)S(1)} %copy-done.7), channel_id=1, source_target_pairs={{16,0},{32,16},{48,32},{64,48},{80,64},{96,80},{112,96},{128,112},... | collective-permute-start | bytes 1376264 | tf_op jit(solution)/shard_map/ppermute | solution.py:20
  17.2 38.9 %collective-permute-start = (bf16[1,64,3584]{2,1,0:T(8,128)(2,1)S(1)}, bf16[1,64,3584]{2,1,0:T(8,128)(2,1)}, u32[]{:S(2)}, u32[]{:S(2)}) collective-permute-start(bf16[1,64,3584]{2,1,0:T(8,128)(2,1)S(1)} %copy-done.8), channel_id=1, source_target_pairs={{0,16},{16,32},{32,48},{48,64},{64,80},{80,96},{96,112},{112,128},... | collective-permute-start | bytes 1376264 | tf_op jit(solution)/shard_map/ppermute | solution.py:20
  44.7 3.5 copy-start.3
  48.2 23.4 %all-to-all-start.3 = ((bf16[16,40,448]{2,1,0:T(8,128)(2,1)}), bf16[16,40,448]{2,1,0:T(8,128)(2,1)S(1)}, u32[]{:S(2)}, u32[]{:S(2)}) async-start(bf16[16,40,448]{2,1,0:T(8,128)(2,1)} %bitcast.25), calls=%async_computation.3 | async-start | bytes 1310720 | tf_op jit(solution)/shard_map/all_to_all | solution.py:133
  57.1 6.1 %copy-start.5 = (bf16[1,64,3584]{2,1,0:T(8,128)(2,1)}, bf16[1,64,3584]{2,1,0:T(8,128)(2,1)S(1)}, u32[]{:S(2)}) copy-start(bf16[1,64,3584]{2,1,0:T(8,128)(2,1)S(1)} %broadcast_select_fusion.1) | copy-start | bytes 1376260
  71.5 8.1 %copy-start.2 = (bf16[16,40,448]{2,1,0:T(8,128)(2,1)}, bf16[16,40,448]{2,1,0:T(8,128)(2,1)S(1)}, u32[]{:S(2)}) copy-start(bf16[16,40,448]{2,1,0:T(8,128)(2,1)S(1)} %all-to-all-done.3) | copy-start | bytes 1720324
  71.5 24.6 %all-to-all-start = ((bf16[16,40,448]{2,1,0:T(8,128)(2,1)}), bf16[16,40,448]{2,1,0:T(8,128)(2,1)}, u32[]{:S(2)}, u32[]{:S(2)}) async-start(bf16[16,40,448]{2,1,0:T(8,128)(2,1)} %bitcast.5), calls=%async_computation | async-start | bytes 1310720 | tf_op jit(solution)/shard_map/all_to_all | solution.py:116
  83.9 50.7 %collective-permute-start.8 = (bf16[320,3072]{1,0:T(8,128)(2,1)}, bf16[320,3072]{1,0:T(8,128)(2,1)}, u32[]{:S(2)}, u32[]{:S(2)}) collective-permute-start(bf16[320,3072]{1,0:T(8,128)(2,1)} %select_convert_fusion), channel_id=1, source_target_pairs={{0,1},{1,0},{2,3},{3,2},{4,5},{5,4},{6,7},{7,6},{8,9},{9,8},{10,11... | collective-permute-start | bytes 5898248 | tf_op jit(solution)/shard_map/ppermute | solution.py:14
  96.2 38.4 %slice-start = ((s8[5242880]{0:T(1024)(128)(4,1)}), s8[4194304]{0:T(1024)(128)(4,1)S(1)}, s32[]{:S(2)}) async-start(s8[5242880]{0:T(1024)(128)(4,1)} %bitcast.67), calls=%async_computation.5 | async-start | bytes 8388608
  96.2 38.4 %slice-start.1 = ((s8[5242880]{0:T(1024)(128)(4,1)}), s8[1048576]{0:T(1024)(128)(4,1)S(1)}, s32[]{:S(2)}) async-start(s8[5242880]{0:T(1024)(128)(4,1)} %bitcast.67), calls=%async_computation.6 | async-start | bytes 2097152
  99.8 83.2 %collective-permute-start.1 = (bf16[320,2048]{1,0:T(8,128)(2,1)S(1)}, bf16[320,2048]{1,0:T(8,128)(2,1)S(1)}, u32[]{:S(2)}, u32[]{:S(2)}) collective-permute-start(bf16[320,2048]{1,0:T(8,128)(2,1)S(1)} %select_convert_fusion.1), channel_id=1, source_target_pairs={{0,1},{1,0},{2,3},{3,2},{4,5},{5,4},{6,7},{7,6},{8,9},{9,8},{10,11... | collective-permute-start | bytes 3932168 | tf_op jit(solution)/shard_map/ppermute | solution.py:14
  136.8 49.5 %collective-permute-start.9 = (bf16[160,3072]{1,0:T(8,128)(2,1)S(1)}, bf16[160,3072]{1,0:T(8,128)(2,1)S(1)}, u32[]{:S(2)}, u32[]{:S(2)}) collective-permute-start(bf16[160,3072]{1,0:T(8,128)(2,1)S(1)} %select_convert_fusion.2), channel_id=1, source_target_pairs={{0,2},{1,3},{2,0},{3,1},{4,6},{5,7},{6,4},{7,5},{8,10},{9,11},{10,... | collective-permute-start | bytes 2949128 | tf_op jit(solution)/shard_map/ppermute | solution.py:14
  183.9 33.3 %collective-permute-start.2 = (bf16[160,2048]{1,0:T(8,128)(2,1)S(1)}, bf16[160,2048]{1,0:T(8,128)(2,1)S(1)}, u32[]{:S(2)}, u32[]{:S(2)}) collective-permute-start(bf16[160,2048]{1,0:T(8,128)(2,1)S(1)} %select_convert_fusion.3), channel_id=1, source_target_pairs={{0,2},{1,3},{2,0},{3,1},{4,6},{5,7},{6,4},{7,5},{8,10},{9,11},{10,... | collective-permute-start | bytes 1966088 | tf_op jit(solution)/shard_map/ppermute | solution.py:14
  186.7 33.3 %collective-permute-start.10 = (bf16[80,3072]{1,0:T(8,128)(2,1)S(1)}, bf16[80,3072]{1,0:T(8,128)(2,1)S(1)}, u32[]{:S(2)}, u32[]{:S(2)}) collective-permute-start(bf16[80,3072]{1,0:T(8,128)(2,1)S(1)} %select_convert_fusion.4), channel_id=1, source_target_pairs={{0,4},{1,5},{2,6},{3,7},{4,0},{5,1},{6,2},{7,3},{8,12},{9,13},{10,... | collective-permute-start | bytes 1474568 | tf_op jit(solution)/shard_map/ppermute | solution.py:14
  217.5 12.5 %collective-permute-start.3 = (bf16[80,2048]{1,0:T(8,128)(2,1)S(1)}, bf16[80,2048]{1,0:T(8,128)(2,1)S(1)}, u32[]{:S(2)}, u32[]{:S(2)}) collective-permute-start(bf16[80,2048]{1,0:T(8,128)(2,1)S(1)} %select_convert_fusion.5), channel_id=1, source_target_pairs={{0,4},{1,5},{2,6},{3,7},{4,0},{5,1},{6,2},{7,3},{8,12},{9,13},{10,... | collective-permute-start | bytes 983048 | tf_op jit(solution)/shard_map/ppermute | solution.py:14
  220.4 16.7 %collective-permute-start.11 = (bf16[80,2048]{1,0:T(8,128)(2,1)S(1)}, bf16[80,2048]{1,0:T(8,128)(2,1)S(1)}, u32[]{:S(2)}, u32[]{:S(2)}) collective-permute-start(bf16[80,2048]{1,0:T(8,128)(2,1)S(1)} %pad_maximum_fusion.5), channel_id=1, source_target_pairs={{0,4},{1,5},{2,6},{3,7},{4,0},{5,1},{6,2},{7,3},{8,12},{9,13},{10,... | collective-permute-start | bytes 983048 | tf_op jit(solution)/shard_map/ppermute | solution.py:14
  230.2 9.4 %collective-permute-start.4 = (bf16[80,1024]{1,0:T(8,128)(2,1)S(1)}, bf16[80,1024]{1,0:T(8,128)(2,1)S(1)}, u32[]{:S(2)}, u32[]{:S(2)}) collective-permute-start(bf16[80,1024]{1,0:T(8,128)(2,1)S(1)} %fusion.29), channel_id=1, source_target_pairs={{0,4},{1,5},{2,6},{3,7},{4,0},{5,1},{6,2},{7,3},{8,12},{9,13},{10,... | collective-permute-start | bytes 491528 | tf_op jit(solution)/shard_map/ppermute | solution.py:14
  237.1 46.9 %collective-permute-start.12 = (bf16[160,2048]{1,0:T(8,128)(2,1)S(1)}, bf16[160,2048]{1,0:T(8,128)(2,1)S(1)}, u32[]{:S(2)}, u32[]{:S(2)}) collective-permute-start(bf16[160,2048]{1,0:T(8,128)(2,1)S(1)} %maximum_select_fusion.8), channel_id=1, source_target_pairs={{0,2},{1,3},{2,0},{3,1},{4,6},{5,7},{6,4},{7,5},{8,10},{9,11},{10,... | collective-permute-start | bytes 1966088 | tf_op jit(solution)/shard_map/ppermute | solution.py:14
  239.7 42.3 %collective-permute-start.5 = (bf16[160,1024]{1,0:T(8,128)(2,1)S(1)}, bf16[160,1024]{1,0:T(8,128)(2,1)S(1)}, u32[]{:S(2)}, u32[]{:S(2)}) collective-permute-start(bf16[160,1024]{1,0:T(8,128)(2,1)S(1)} %maximum_select_fusion.9), channel_id=1, source_target_pairs={{0,2},{1,3},{2,0},{3,1},{4,6},{5,7},{6,4},{7,5},{8,10},{9,11},{10,... | collective-permute-start | bytes 983048 | tf_op jit(solution)/shard_map/ppermute | solution.py:14
  282.2 19.5 %collective-permute-start.6 = (bf16[320,1024]{1,0:T(8,128)(2,1)S(1)}, bf16[320,1024]{1,0:T(8,128)(2,1)S(1)}, u32[]{:S(2)}, u32[]{:S(2)}) collective-permute-start(bf16[320,1024]{1,0:T(8,128)(2,1)S(1)} %maximum_select_fusion.7), channel_id=1, source_target_pairs={{0,1},{1,0},{2,3},{3,2},{4,5},{5,4},{6,7},{7,6},{8,9},{9,8},{10,11... | collective-permute-start | bytes 1966088 | tf_op jit(solution)/shard_map/ppermute | solution.py:14
  285.6 48.4 %collective-permute-start.13 = (bf16[320,2048]{1,0:T(8,128)(2,1)}, bf16[320,2048]{1,0:T(8,128)(2,1)}, u32[]{:S(2)}, u32[]{:S(2)}) collective-permute-start(bf16[320,2048]{1,0:T(8,128)(2,1)} %maximum_select_fusion.6), channel_id=1, source_target_pairs={{0,1},{1,0},{2,3},{3,2},{4,5},{5,4},{6,7},{7,6},{8,9},{9,8},{10,11... | collective-permute-start | bytes 3932168 | tf_op jit(solution)/shard_map/ppermute | solution.py:14
  302.6 8.7 %copy-start.9 = (s32[1,64,1]{1,2,0:T(1,128)S(1)}, s32[1,64,1]{1,2,0:T(1,128)}, u32[]{:S(2)}) copy-start(s32[1,64,1]{1,2,0:T(1,128)} %param.18) | copy-start | bytes 772
  303.7 36.9 %all-to-all-start.1 = ((bf16[16,40,448]{2,1,0:T(8,128)(2,1)}), bf16[16,40,448]{2,1,0:T(8,128)(2,1)S(1)}, u32[]{:S(2)}, u32[]{:S(2)}) async-start(bf16[16,40,448]{2,1,0:T(8,128)(2,1)} %bitcast.10), calls=%async_computation.1 | async-start | bytes 1310720 | tf_op jit(solution)/shard_map/all_to_all | solution.py:123
  340.6 20.7 %all-to-all-start.4 = ((bf16[16,40,448]{2,1,0:T(8,128)(2,1)}), bf16[16,40,448]{2,1,0:T(8,128)(2,1)S(1)}, u32[]{:S(2)}, u32[]{:S(2)}) async-start(bf16[16,40,448]{2,1,0:T(8,128)(2,1)} %bitcast.27), calls=%async_computation.4 | async-start | bytes 1310720 | tf_op jit(solution)/shard_map/all_to_all | solution.py:146
  348.0 3.4 copy-start.11
  352.3 10.4 %copy-start.4 = (bf16[1,64,3584]{2,1,0:T(8,128)(2,1)S(1)}, bf16[1,64,3584]{2,1,0:T(8,128)(2,1)}, u32[]{:S(2)}) copy-start(bf16[1,64,3584]{2,1,0:T(8,128)(2,1)} %copy-done.3) | copy-start | bytes 1376260
  352.3 10.4 %copy-start.12 = (f32[1,64,1]{1,2,0:T(1,128)S(1)}, f32[1,64,1]{1,2,0:T(1,128)}, u32[]{:S(2)}) copy-start(f32[1,64,1]{1,2,0:T(1,128)} %param.19) | copy-start | bytes 772
  (4 other events, 9.0 us)
where the time goes:
time: 369 us; the launch traced here: 364 us
  waiting for transfers between devices  241 us (65%)
  starting transfers between devices  77.2 us (21%)
  matrix products  17 us (5%)
  other arithmetic  15 us (4%)
  local copies, waits for them, and re-layouts  12.6 us (3%)
    ppermute x12, waiting for transfers between devices, partner(): return lax.ppermute(value, axis, pairs)  187 us
    ppermute x12, starting transfers between devices, partner(): return lax.ppermute(value, axis, pairs)  33.3 us
    ppermute x2, waiting for transfers between devices, shifted(): return lax.ppermute(x, axis, pairs)  24.2 us
    all_to_all x2, starting transfers between devices, body(): lax.all_to_all(produced.reshape(source_count, slot_count, width), 'expert...  14.9 us
    all_to_all x1, waiting for transfers between devices, body(): lax.all_to_all(send_fwd, 'expert', split_axis=0, concat_axis=0, tiled=True)  9.78 us
    all_to_all x2, waiting for transfers between devices, body(): lax.all_to_all(produced.reshape(source_count, slot_count, width), 'expert...  9.77 us
    all_to_all x1, waiting for transfers between devices, body(): lax.all_to_all(send_grad, 'expert', split_axis=0, concat_axis=0, tiled=True)  8.26 us
    all_to_all x1, starting transfers between devices, body(): lax.all_to_all(send_fwd, 'expert', split_axis=0, concat_axis=0, tiled=True)  8.12 us
  transfers between devices with their start and end apart: 19, of which 15 were waited for; matrix products, arithmetic and copies ran while one was open for 10% of the time, Pallas kernels for 0%

commit v1 on v0

v1 whole, which is shorter than its diff:
```python
import functools

import jax
import jax.numpy as jnp
from jax import lax
from jax.experimental import pallas as pl
from jax.experimental.pallas import tpu as pltpu
from jax.sharding import PartitionSpec as P

XN = 4
YN = 4
CHUNKS = 4
MESH = pl.DeviceIdType.MESH
NT = (((1,), (1,)), ((), ()))


def kernel(
    sections,
    fwd_slabs,
    bwd_slabs,
    grad_slabs,
    w_gate,
    w_up,
    w_down,
    aux_in,
    fwd_ret,
    bwd_ret,
    gu,
    dn,
    xf,
    xb,
    xg,
    aux,
    xcat,
    gcat,
    s1_out,
    s1_in,
    s2_out,
    s2_in,
    kept,
    s1d_out,
    s1d_in,
    s2d_out,
    s2d_in,
    keptd,
    hid,
    back,
    grads,
    out_acc,
    grad_acc,
    out_send,
    grad_send,
    wdir_send,
    wdir_recv,
    wrel_send,
    wrel_recv,
    wloc,
    disp_send,
    disp_recv,
    s_send,
    s_recv,
    ag_send,
    ag_recv,
    ret_send,
    ret_recv,
):
    section = lax.axis_index("pipe")
    me = lax.axis_index("expert")
    x = me // YN
    y = me % YN
    parity = y % 2
    high = y // 2
    place = parity * 2 + high
    slots = gu.shape[0]
    chunk = dn.shape[3]
    width = dn.shape[2]
    half_rows = width // 2
    full = 2 * width
    last = sections - 1

    def column(k, pipe=None):
        return (section if pipe is None else pipe, x * YN + (y + k) % YN)

    def row(k):
        return (section, (x + k) % XN * YN + y)

    near = (section, x * YN + y + 1 - 2 * parity)
    far = (section, x * YN + (y + 2) % YN)

    barrier = pltpu.get_barrier_semaphore()

    def greet(device):
        pl.semaphore_signal(barrier, inc=1, device_id=device, device_id_type=MESH)

    for k in range(1, YN):
        greet(column(k))
    greet(row(1))
    greet(row(XN - 1))

    @pl.when(section < last)
    def _():
        for k in range(YN):
            greet(column(k, section + 1))

    @pl.when(section > 0)
    def _():
        for k in range(YN):
            greet(column(k, section - 1))

    inner = jnp.where(section < last, YN, 0) + jnp.where(section > 0, YN, 0)
    pl.semaphore_wait(barrier, YN + 1 + inner)

    ending = []

    def send(src, dst, send_sem, recv_sem, device):
        copy = pltpu.make_async_remote_copy(
            src_ref=src,
            dst_ref=dst,
            send_sem=send_sem,
            recv_sem=recv_sem,
            device_id=device,
            device_id_type=MESH,
        )
        copy.start()
        return copy

    def sent(*args):
        ending.append(send(*args))

    def arrive(dst, sem):
        pltpu.make_async_copy(dst, dst, sem).wait()

    items = 2 * slots
    ways = ((1, 0), (XN - 1, 1))

    def parts(i, source):
        f = i % slots
        if i < slots:
            return [gu.at[f, source, :, pl.ds(0, chunk)], gu.at[f, source, :, pl.ds(chunk, chunk)]]
        return [dn.at[f, source]]

    def own_refs(i):
        f = i % slots
        span = pl.ds(f * chunk, chunk)
        if i < slots:
            return [w_gate.at[:, span], w_up.at[:, span]]
        return [w_down.at[:, span]]

    def own_send(i):
        for part, (src, dst) in enumerate(zip(own_refs(i), parts(i, x))):
            for k, way in ways:
                sent(src, dst, wdir_send.at[i, way, part], wdir_recv.at[i, way, part], row(k))

    def direct_wait(i):
        for k, way in ways:
            for part, dst in enumerate(parts(i, (x + XN - k) % XN)):
                arrive(dst, wdir_recv.at[i, way, part])

    def relay_ref(i, source, way):
        f = i % slots
        rows = pl.ds(way * half_rows, half_rows)
        return gu.at[f, source, rows] if i < slots else dn.at[f, source, rows]

    def relay(i):
        for k, way in ways:
            ref = relay_ref(i, (x + XN - k) % XN, way)
            sent(ref, ref, wrel_send.at[i, way], wrel_recv.at[i, way], row(k))

    def relay_wait(i):
        for _, way in ways:
            arrive(relay_ref(i, (x + 2) % XN, way), wrel_recv.at[i, way])

    own_send(0)
    own_send(1)
    locals_ = []
    for i in range(items):
        for part, (src, dst) in enumerate(zip(own_refs(i), parts(i, x))):
            copy = pltpu.make_async_copy(src, dst, wloc.at[i, part])
            copy.start()
            locals_.append((i, copy))

    def spread(number, slabs, buffer, sems_out, sems_in):
        for k in range(1, YN):
            sent(
                slabs.at[(y + k) % YN] if slabs is not aux_in else slabs,
                buffer.at[place],
                sems_out.at[number, k],
                sems_in.at[number, k],
                column(k),
            )
        pltpu.make_async_copy(
            slabs.at[y] if slabs is not aux_in else slabs, buffer.at[place], sems_in.at[number, 0]
        ).start()

    def shifted(number, slabs, buffer, step, edge):
        def copies(target):
            return [
                pltpu.make_async_remote_copy(
                    src_ref=slabs.at[(y + k) % YN],
                    dst_ref=buffer.at[place],
                    send_sem=disp_send.at[number, k],
                    recv_sem=disp_recv.at[number, k],
                    device_id=column(k, target),
                    device_id_type=MESH,
                )
                for k in range(YN)
            ]

        def own():
            return [
                pltpu.make_async_remote_copy(
                    src_ref=slabs.at[(y + k) % YN],
                    dst_ref=buffer.at[place],
                    send_sem=disp_send.at[number, YN + k],
                    recv_sem=disp_recv.at[number, k],
                    device_id=column(k),
                    device_id_type=MESH,
                )
                for k in range(1, YN)
            ]

        stays = last if step > 0 else 0

        @pl.when(section != stays)
        def _():
            for copy in copies(section + step):
                copy.start()

        @pl.when(section == edge)
        def _():
            for copy in own():
                copy.start()
            pltpu.make_async_copy(slabs.at[y], buffer.at[place], disp_recv.at[number, 0]).start()

        def finish():
            @pl.when(section != stays)
            def _():
                for copy in copies(section + step):
                    copy.wait_send()

            @pl.when(section == edge)
            def _():
                for copy in own():
                    copy.wait_send()

        return finish

    def place_of(k):
        other = (y + YN - k) % YN
        return other % 2 * 2 + other // 2

    def spread_wait(number, buffer):
        for k in range(YN):
            arrive(buffer.at[place_of(k)], disp_recv.at[number, k])

    spread(0, aux_in, aux, disp_send, disp_recv)
    fwd_finish = shifted(1, fwd_slabs, xf, 1, 0)
    spread(2, bwd_slabs, xb, disp_send, disp_recv)
    grad_finish = shifted(3, grad_slabs, xg, -1, last)

    direct_wait(0)
    relay(0)
    if items > 2:
        own_send(2)

    spread_wait(0, aux)
    fwd_first = [aux[q, :, 0:1] < 0.5 for q in range(YN)]
    bwd_first = [aux[q, :, 2:3] < 0.5 for q in range(YN)]

    def divide(block, first, target):
        zero = jnp.zeros_like(block)
        target[:, pl.ds(0, full)] = jnp.where(first, block, zero)
        target[:, pl.ds(full, full)] = jnp.where(first, zero, block)

    spread_wait(1, xf)
    for q in range(YN):
        divide(xf[q], fwd_first[q], xcat.at[q // 2, 0, q % 2])
    spread_wait(2, xb)
    for q in range(YN):
        divide(xb[q], bwd_first[q], xcat.at[q // 2, 1, q % 2])

    tokens = xf.shape[1]

    def gather_send(i, ref):
        for k in range(1, YN):
            sent(ref, ref, ag_send.at[i, k - 1], ag_recv.at[i, k - 1], column(k))

    def gather_wait(i, buffer):
        for k in range(1, YN):
            arrive(buffer.at[place_of(k)], ag_recv.at[i, k - 1])

    def first_stage(i):
        f = i % slots
        if i < slots:
            mats = gu[f].reshape(XN * width, 2 * chunk)
            rows = xcat.at[1 - parity][...].reshape(4 * tokens, 2 * full)
            given = jnp.dot(rows, mats, preferred_element_type=jnp.float32)
            s1_out[f] = given.astype(jnp.bfloat16).reshape(s1_out.shape[1:])
            sent(s1_out.at[f], s1_in.at[f], s_send.at[i, 0], s_recv.at[i, 0], near)
            rows = xcat.at[parity][...].reshape(4 * tokens, 2 * full)
            own = jnp.dot(rows, mats, preferred_element_type=jnp.float32)
            kept[f] = own.reshape(kept.shape[1:])
        else:
            mats = dn[f].reshape(XN * width, chunk)
            rows = gcat.at[1 - parity][...].reshape(2 * tokens, 2 * full)
            given = jnp.dot(rows, mats, preferred_element_type=jnp.float32)
            s1d_out[f] = given.astype(jnp.bfloat16).reshape(s1d_out.shape[1:])
            sent(s1d_out.at[f], s1d_in.at[f], s_send.at[i, 0], s_recv.at[i, 0], near)
            rows = gcat.at[parity][...].reshape(2 * tokens, 2 * full)
            own = jnp.dot(rows, mats, preferred_element_type=jnp.float32)
            keptd[f] = own.reshape(keptd.shape[1:])

    def second_stage(i):
        f = i % slots
        if i < slots:
            arrive(s1_in.at[f], s_recv.at[i, 0])
            for b in range(2):
                total = kept[f, b, 1 - high] + s1_in[f, b, 1 - high].astype(jnp.float32)
                s2_out[f, b] = total.astype(jnp.bfloat16)
            sent(s2_out.at[f], s2_in.at[f], s_send.at[i, 1], s_recv.at[i, 1], far)
        else:
            arrive(s1d_in.at[f], s_recv.at[i, 0])
            total = keptd[f, 1 - high] + s1d_in[f, 1 - high].astype(jnp.float32)
            s2d_out[f] = total.astype(jnp.bfloat16)
            sent(s2d_out.at[f], s2d_in.at[f], s_send.at[i, 1], s_recv.at[i, 1], far)

    def third_stage(i):
        f = i % slots
        if i < slots:
            arrive(s2_in.at[f], s_recv.at[i, 1])
            sums = [
                kept[f, b, high]
                + s1_in[f, b, high].astype(jnp.float32)
                + s2_in[f, b].astype(jnp.float32)
                for b in range(2)
            ]
            back[f] = sums[1]
            gate, up = sums[0][:, :chunk], sums[0][:, chunk:]
            hid[f, place] = (gate * jax.nn.sigmoid(gate) * up).astype(jnp.bfloat16)
            gather_send(i, hid.at[f, place])
        else:
            arrive(s2d_in.at[f], s_recv.at[i, 1])
            grad_hidden = (
                keptd[f, high]
                + s1d_in[f, high].astype(jnp.float32)
                + s2d_in[f].astype(jnp.float32)
            )
            gate, up = back[f, :, :chunk], back[f, :, chunk:]
            sig = jax.nn.sigmoid(gate)
            grad_gate = grad_hidden * up * sig * (1.0 + gate * (1.0 - sig))
            grad_up = grad_hidden * (gate * sig)
            grads[f, place, :, pl.ds(0, chunk)] = grad_gate.astype(jnp.bfloat16)
            grads[f, place, :, pl.ds(chunk, chunk)] = grad_up.astype(jnp.bfloat16)
            gather_send(i, grads.at[f, place])

    def accumulate(values, first, mats, acc, start):
        zero = jnp.zeros_like(values[0])
        zeroth = jnp.concatenate([jnp.where(m, v, zero) for m, v in zip(first, values)], axis=0)
        other = jnp.concatenate([jnp.where(m, zero, v) for m, v in zip(first, values)], axis=0)
        total = lax.dot_general(zeroth, mats[:full], NT, preferred_element_type=jnp.float32)
        total += lax.dot_general(other, mats[full:], NT, preferred_element_type=jnp.float32)
        if start:
            acc[...] = total
        else:
            acc[...] += total

    def forward_sum(f):
        gather_wait(f, hid.at[f])
        mats = dn[f].reshape(XN * width, chunk)
        accumulate([hid[f, q] for q in range(YN)], fwd_first, mats, out_acc, f == 0)

    def backward_sum(f):
        gather_wait(slots + f, grads.at[f])
        mats = gu[f].reshape(XN * width, 2 * chunk)
        accumulate([grads[f, q] for q in range(YN)], bwd_first, mats, grad_acc, f == 0)

    def give_back(number, residual, acc, lane, buffer, result):
        for q in range(YN):
            produced = acc[pl.ds(q * tokens, tokens), :].astype(jnp.bfloat16).astype(jnp.float32)
            weight = aux[q, :, lane : lane + 1]
            buffer[q] = (residual[q].astype(jnp.float32) + weight * produced).astype(jnp.bfloat16)
        for k in range(1, YN):
            other = (y + k) % YN
            sent(
                buffer.at[other % 2 * 2 + other // 2],
                result.at[y],
                ret_send.at[number, k],
                ret_recv.at[number, k],
                column(k),
            )
        pltpu.make_async_copy(buffer.at[place], result.at[y], ret_recv.at[number, 0]).start()

    def give_wait(number, result):
        for k in range(YN):
            arrive(result.at[(y + YN - k) % YN], ret_recv.at[number, k])

    for i in range(items):
        f = i % slots
        if i + 1 < items:
            direct_wait(i + 1)
            relay(i + 1)
            if i + 3 < items:
                own_send(i + 3)
        relay_wait(i)
        for number, copy in locals_:
            if number == i:
                copy.wait()
        if i == slots:
            spread_wait(3, xg)
            for q in range(YN):
                divide(xg[q], bwd_first[q], gcat.at[q // 2, q % 2])
        first_stage(i)
        if i > 0:
            third_stage(i - 1)
        if i >= slots and f >= 1:
            forward_sum(f - 1)
        second_stage(i)
        if i >= slots and f >= 2:
            backward_sum(f - 2)

    forward_sum(slots - 1)
    third_stage(items - 1)
    give_back(0, xf, out_acc, 1, out_send, fwd_ret)
    if slots >= 2:
        backward_sum(slots - 2)
    backward_sum(slots - 1)
    give_back(1, xg, grad_acc, 3, grad_send, bwd_ret)
    give_wait(0, fwd_ret)
    give_wait(1, bwd_ret)
    for copy in ending:
        copy.wait_send()
    fwd_finish()
    grad_finish()


def fused(fwd_slabs, bwd_slabs, grad_slabs, w_gate, w_up, w_down, aux, sections):
    _, tokens, full = fwd_slabs.shape
    width, units = w_gate.shape
    slots = CHUNKS
    chunk = units // slots
    rows = YN * tokens
    bf16, f32 = jnp.bfloat16, jnp.float32
    dma = pltpu.SemaphoreType.DMA
    items = 2 * slots
    slab = jax.ShapeDtypeStruct((YN, tokens, full), bf16)
    return pl.pallas_call(
        functools.partial(kernel, sections),
        out_shape=(slab, slab),
        in_specs=[pl.BlockSpec(memory_space=pl.ANY)] * 7,
        out_specs=(pl.BlockSpec(memory_space=pl.ANY),) * 2,
        scratch_shapes=[
            pltpu.VMEM((slots, XN, width, 2 * chunk), bf16),
            pltpu.VMEM((slots, XN, width, chunk), bf16),
            pltpu.VMEM((YN, tokens, full), bf16),
            pltpu.VMEM((YN, tokens, full), bf16),
            pltpu.VMEM((YN, tokens, full), bf16),
            pltpu.VMEM((YN, tokens, 128), f32),
            pltpu.VMEM((2, 2, 2, tokens, 2 * full), bf16),
            pltpu.VMEM((2, 2, tokens, 2 * full), bf16),
            pltpu.VMEM((slots, 2, 2, tokens, 2 * chunk), bf16),
            pltpu.VMEM((slots, 2, 2, tokens, 2 * chunk), bf16),
            pltpu.VMEM((slots, 2, tokens, 2 * chunk), bf16),
            pltpu.VMEM((slots, 2, tokens, 2 * chunk), bf16),
            pltpu.VMEM((slots, 2, 2, tokens, 2 * chunk), f32),
            pltpu.VMEM((slots, 2, tokens, chunk), bf16),
            pltpu.VMEM((slots, 2, tokens, chunk), bf16),
            pltpu.VMEM((slots, tokens, chunk), bf16),
            pltpu.VMEM((slots, tokens, chunk), bf16),
            pltpu.VMEM((slots, 2, tokens, chunk), f32),
            pltpu.VMEM((slots, YN, tokens, chunk), bf16),
            pltpu.VMEM((slots, tokens, 2 * chunk), f32),
            pltpu.VMEM((slots, YN, tokens, 2 * chunk), bf16),
            pltpu.VMEM((rows, full), f32),
            pltpu.VMEM((rows, full), f32),
            pltpu.VMEM((YN, tokens, full), bf16),
            pltpu.VMEM((YN, tokens, full), bf16),
            dma((items, 2, 2)),
            dma((items, 2, 2)),
            dma((items, 2)),
            dma((items, 2)),
            dma((items, 2)),
            dma((4, 2 * YN)),
            dma((4, YN)),
            dma((items, 2)),
            dma((items, 2)),
            dma((items, YN - 1)),
            dma((items, YN - 1)),
            dma((2, YN)),
            dma((2, YN)),
        ],
        compiler_params=pltpu.CompilerParams(
            collective_id=0, has_side_effects=True, vmem_limit_bytes=62 * 1024 * 1024
        ),
    )(fwd_slabs, bwd_slabs, grad_slabs, w_gate, w_up, w_down, aux)


def slabs_of(values):
    tokens, model = values.shape
    cut = values.reshape(tokens, 2, YN, model // (2 * YN))
    return cut.transpose(2, 0, 1, 3).reshape(YN, tokens, model // YN)


def whole_of(slabs):
    _, tokens, full = slabs.shape
    cut = slabs.reshape(YN, tokens, 2, full // 2)
    return cut.transpose(1, 2, 0, 3).reshape(tokens, YN * full)


def body(sections, fwd_in, bwd_in, bwd_grad_in, w_gate, w_up, w_down, fwd_ids, fwd_gates, bwd_ids, bwd_gates):
    f32 = jnp.float32
    aux = jnp.concatenate(
        [fwd_ids[0].astype(f32), fwd_gates[0], bwd_ids[0].astype(f32), bwd_gates[0]], axis=1
    )
    aux = jnp.pad(aux, ((0, 0), (0, 124)))
    fwd, bwd = fused(
        slabs_of(fwd_in[0]),
        slabs_of(bwd_in[0]),
        slabs_of(bwd_grad_in[0]),
        w_gate[0],
        w_up[0],
        w_down[0].T,
        aux,
        sections,
    )
    return whole_of(fwd)[None], whole_of(bwd)[None]


def solution(mesh):
    rows = P("pipe", "expert", None)
    return jax.shard_map(
        functools.partial(body, mesh.shape["pipe"]),
        mesh=mesh,
        in_specs=(rows, rows, rows, rows, rows, P("pipe", None, "expert"), rows, rows, rows, rows),
        out_specs=(rows, rows),
        check_vma=False,
    )
```

time: 369 us -> 167 us (0.45); the launches traced: 364 us -> 166 us
  waiting for transfers between devices: 241 us -> 0 us
  Pallas kernels: 0 us -> 150 us
  starting transfers between devices: 77.2 us -> 0 us
  matrix products: 17 us -> 0 us
  other arithmetic: 15 us -> 0.01 us
    ppermute x14 -> x0, waiting for transfers between devices: 211 us -> none  [the longest x12 187 us: partner(): return lax.ppermute(value, axis, pairs)]
    pallas_call x0 -> x1, Pallas kernels: none -> 150 us  [fused(): pl.pallas_call(functools.partial(kernel, sections), out_shape=(slab, slab...]
    ppermute x14 -> x0, starting transfers between devices: 38.8 us -> none  [the longest x12 33.3 us: partner(): return lax.ppermute(value, axis, pairs)]
    all_to_all x5 -> x0, starting transfers between devices: 38.4 us -> none  [the longest x2 14.9 us: body(): lax.all_to_all(produced.reshape(source_count, slot_count, width), 'expert...]
    all_to_all x5 -> x0, waiting for transfers between devices: 29.3 us -> none  [the longest x1 9.78 us: body(): lax.all_to_all(send_fwd, 'expert', split_axis=0, concat_axis=0, tiled=True)]
    dot_general x8 -> x0, matrix products: 17 us -> none  [the longest x1 4.81 us: body(): jnp.dot(joined, in_mats.T, preferred_element_type=jnp.float32)]
    convert_element_type x12 -> x1, other arithmetic: 5.32 us -> 0.01 us  [body(): bwd_ids[0].astype(f32)]
    convert_element_type x6 -> x0, local copies, waits for them, and re-layouts: 4.93 us -> none  [the longest x2 1.79 us: dispatch_rows(): jnp.einsum('ect,tgk->egck', table, pieces, preferred_element_type=jnp.flo...]
  transfers between devices with their start and end apart: 19 -> 0, of which waited for: 15 -> 0; matrix products, arithmetic and copies ran while one was open for 10% -> 0% of each run, Pallas kernels for 0% -> 0%
where the time goes in v1:
time: 167 us; the launch traced here: 166 us
  Pallas kernels  150 us (90%)
  local copies, waits for them, and re-layouts  15.9 us (10%)
    pallas_call x1, Pallas kernels, fused(): pl.pallas_call(functools.partial(kernel, sections), out_shape=(slab, slab...  150 us
    another operation x6, local copies, waits for them, and re-layouts, slabs_of(): cut = values.reshape(tokens, 2, YN, model // (2 * YN))  4.26 us
    reshape x3, local copies, waits for them, and re-layouts, slabs_of(): return cut.transpose(2, 0, 1, 3).reshape(YN, tokens, model // YN)  3.55 us

profile of v1, /device:TPU:250, one launch (start us, length us, event | category | flops | bytes accessed | tf_op | source)
XLA Modules:
  0.0 166.4 jit_solution(9614625890498578236)
XLA Ops:
  0.6 0.0 copy-start.3
  0.6 0.0 copy-start.4
  0.6 0.6 copy-done.3
  1.3 0.0 copy-done.4
  1.3 0.0 copy-start.5
  1.3 0.0 copy-start.6
  1.3 0.7 copy-done.5
  2.0 0.0 copy-done.6
  2.0 0.1 copy.24
  2.1 0.6 pad.4.aux_in
  2.7 1.7 %reshape_squeeze.9 = bf16[64,2,4,448]{3,2,1,0:T(4,128)(2,1)S(1)} reshape(bf16[1,64,3584]{2,1,0:T(8,128)(2,1)} %param.10) | data formatting | bytes 917504 | tf_op jit(solution)/shard_map/reshape;squeeze | solution.py:499
  4.4 0.4 copy.32
  4.8 0.0 copy-start
  4.8 1.2 reshape.45.fwd_slabs
  6.0 0.0 copy-done
  6.0 0.7 reshape_squeeze.10
  6.7 0.4 copy.31
  7.1 0.0 copy-start.1
  7.1 1.2 reshape.46.bwd_slabs
  8.3 0.0 copy-done.1
  8.3 0.7 reshape_squeeze.11
  9.0 0.4 copy.30
  9.4 1.2 reshape.47.grad_slabs
  10.6 149.8 %shard_map.113 = (bf16[4,64,896]{2,1,0:T(8,128)(2,1)}, bf16[4,64,896]{2,1,0:T(8,128)(2,1)}) custom-call(bf16[4,64,896]{2,1,0:T(8,128)(2,1)} %reshape.45.fwd_slabs, bf16[4,64,896]{2,1,0:T(8,128)(2,1)} %reshape.46.bwd_slabs, bf16[4,64,896]{2,1,0:T(8,128)(2,1)} %reshape.47.grad_slabs, bf16[448,1024]{1,0:T(8,128)(2,1)} %bitcast.27, bf16[448,1024]{1,0:T(8,128)(2,1)} %bitcast.28, ...), custom_call_target="tpu_custom_call" | custom-call | tf_op jit(solution)/shard_map/pallas_call | solution.py:446
  160.4 1.5 reshape.48
  161.8 0.7 copy.25
  162.5 0.0 copy-start.2
  162.5 1.4 broadcast_in_dim_reshape.6
  163.9 0.0 copy-done.2
  163.9 0.4 reshape.49
  164.4 0.7 copy.26
  165.1 1.4 broadcast_in_dim_reshape.7
  (2 shorter events, 0.0 us)
Async XLA Ops:
  0.6 0.7 copy-start.3
  0.6 0.7 copy-start.4
  1.3 0.7 copy-start.5
  1.3 0.7 copy-start.6
  4.8 1.2 copy-start
  7.1 1.2 copy-start.1
  162.5 1.4 copy-start.2

commit v2 on v1

v2 whole, which is shorter than its diff:
```python
import functools

import jax
import jax.numpy as jnp
from jax import lax
from jax.experimental import pallas as pl
from jax.experimental.pallas import tpu as pltpu
from jax.sharding import PartitionSpec as P

XN = 4
YN = 4
GATE_PARTS = (2, 2, 2, 2)
DOWN_PARTS = (2, 2, 2, 1, 1)
MESH = pl.DeviceIdType.MESH
NT = (((1,), (1,)), ((), ()))


class Chunk:
    def __init__(self, start, size, parent=None):
        self.start, self.size, self.parent = start, size, parent


def chunks_of(units):
    step = units // sum(GATE_PARTS)
    gates, start = [], 0
    for size in GATE_PARTS:
        gates.append(Chunk(start * step, size * step))
        start += size
    downs, start = [], 0
    for size in DOWN_PARTS:
        first = start * step
        parent = [n for n, g in enumerate(gates) if g.start <= first < g.start + g.size][0]
        downs.append(Chunk(first, size * step, parent))
        start += size
    return gates, downs


def kernel(sections, gates, downs, *refs):
    (fwd_in, bwd_in, grad_in, w_gate, w_up, w_down, fwd_ids, fwd_gates, bwd_ids, bwd_gates) = refs[:10]
    fwd_out, bwd_out = refs[10:12]
    refs = refs[12:]

    def take(count):
        nonlocal refs
        taken, refs = refs[:count], refs[count:]
        return taken

    ng, nd = len(gates), len(downs)
    gu, s1_out, s1_in, s2_out, s2_in, kept, hid, back = [take(ng) for _ in range(8)]
    dn, s1d_out, s1d_in, s2d_out, s2d_in, keptd, grads = [take(nd) for _ in range(7)]
    (whole, small, slab, aux_in, aux, land, xcat, gcat) = take(8)
    (out_acc, grad_acc, ret_out, ret_in) = take(4)
    (load, wdir_send, wdir_recv, wrel_send, wrel_recv, wloc) = take(6)
    (disp_send, disp_recv, s_send, s_recv, ag_send, ag_recv, ret_send, ret_recv, store) = take(9)
    xf, xb, xg = land.at[0], land.at[1], land.at[2]

    section = lax.axis_index("pipe")
    me = lax.axis_index("expert")
    x = me // YN
    y = me % YN
    parity = y % 2
    high = y // 2
    place = parity * 2 + high
    tokens = fwd_in.shape[0]
    width = w_gate.shape[0]
    half_rows = width // 2
    full = 2 * width
    last = sections - 1

    loads = []
    for n, (src, dst) in enumerate(
        [(fwd_in, whole.at[0]), (bwd_in, whole.at[1]), (grad_in, whole.at[2])]
        + [(ref, small.at[j]) for j, ref in enumerate((fwd_ids, fwd_gates, bwd_ids, bwd_gates))]
    ):
        loads.append(pltpu.make_async_copy(src, dst, load.at[n]))
        loads[-1].start()

    def column(k, pipe=None):
        return (section if pipe is None else pipe, x * YN + (y + k) % YN)

    def row(k):
        return (section, (x + k) % XN * YN + y)

    near = (section, x * YN + y + 1 - 2 * parity)
    far = (section, x * YN + (y + 2) % YN)

    barrier = pltpu.get_barrier_semaphore()

    def greet(device):
        pl.semaphore_signal(barrier, inc=1, device_id=device, device_id_type=MESH)

    @pl.when(section < last)
    def _():
        for k in range(YN):
            greet(column(k, section + 1))

    @pl.when(section > 0)
    def _():
        for k in range(YN):
            greet(column(k, section - 1))

    for k in range(1, YN):
        greet(column(k))
    greet(row(1))
    greet(row(XN - 1))

    def cut(n):
        loads[n].wait()
        for t in range(YN):
            slab[n, t] = jnp.concatenate(
                [
                    whole[n, :, t * width : (t + 1) * width],
                    whole[n, :, (YN + t) * width : (YN + t + 1) * width],
                ],
                axis=1,
            )

    for n in range(3, 7):
        loads[n].wait()
    eye = lax.broadcasted_iota(jnp.int32, (tokens, tokens), 0) == lax.broadcasted_iota(
        jnp.int32, (tokens, tokens), 1
    )
    lane = lax.broadcasted_iota(jnp.int32, (tokens, 128), 1)
    table = jnp.zeros((tokens, 128), jnp.float32)
    for j in range(4):
        line = jnp.broadcast_to(small[j], (tokens, tokens))
        stood = jnp.sum(jnp.where(eye, line, 0.0), axis=1, keepdims=True)
        table = jnp.where(lane == j, stood, table)
    aux_in[...] = table
    cut(0)
    cut(1)

    inner = jnp.where(section < last, YN, 0) + jnp.where(section > 0, YN, 0)
    pl.semaphore_wait(barrier, YN + 1 + inner)

    ending = []

    def send(src, dst, send_sem, recv_sem, device):
        copy = pltpu.make_async_remote_copy(
            src_ref=src,
            dst_ref=dst,
            send_sem=send_sem,
            recv_sem=recv_sem,
            device_id=device,
            device_id_type=MESH,
        )
        copy.start()
        return copy

    def sent(*args):
        ending.append(send(*args))

    def arrive(dst, sem):
        pltpu.make_async_copy(dst, dst, sem).wait()

    items = ng + nd
    ways = ((1, 0), (XN - 1, 1))

    def parts(i, source):
        if i < ng:
            c = gates[i].size
            return [gu[i].at[source, :, pl.ds(0, c)], gu[i].at[source, :, pl.ds(c, c)]]
        return [dn[i - ng].at[source]]

    def own_refs(i):
        c = gates[i] if i < ng else downs[i - ng]
        span = pl.ds(c.start, c.size)
        return [w_gate.at[:, span], w_up.at[:, span]] if i < ng else [w_down.at[:, span]]

    def own_send(i):
        if i >= items:
            return
        for part, (src, dst) in enumerate(zip(own_refs(i), parts(i, x))):
            for k, way in ways:
                sent(src, dst, wdir_send.at[i, way, part], wdir_recv.at[i, way, part], row(k))

    def direct_wait(i):
        for k, way in ways:
            for part, dst in enumerate(parts(i, (x + XN - k) % XN)):
                arrive(dst, wdir_recv.at[i, way, part])

    def relay_ref(i, source, way):
        rows = pl.ds(way * half_rows, half_rows)
        return gu[i].at[source, rows] if i < ng else dn[i - ng].at[source, rows]

    def relay(i):
        for k, way in ways:
            ref = relay_ref(i, (x + XN - k) % XN, way)
            sent(ref, ref, wrel_send.at[i, way], wrel_recv.at[i, way], row(k))

    def relay_wait(i):
        for _, way in ways:
            arrive(relay_ref(i, (x + 2) % XN, way), wrel_recv.at[i, way])

    own_send(0)
    own_send(1)

    def spread(number, source, buffer):
        for k in range(1, YN):
            sent(
                source(k),
                buffer.at[place],
                disp_send.at[number, k],
                disp_recv.at[number, k],
                column(k),
            )
        pltpu.make_async_copy(source(0), buffer.at[place], disp_recv.at[number, 0]).start()

    def shifted(number, n, buffer, step, edge):
        def copies(target):
            return [
                pltpu.make_async_remote_copy(
                    src_ref=slab.at[n, (y + k) % YN],
                    dst_ref=buffer.at[place],
                    send_sem=disp_send.at[number, k],
                    recv_sem=disp_recv.at[number, k],
                    device_id=column(k, target),
                    device_id_type=MESH,
                )
                for k in range(YN)
            ]

        def own():
            return [
                pltpu.make_async_remote_copy(
                    src_ref=slab.at[n, (y + k) % YN],
                    dst_ref=buffer.at[place],
                    send_sem=disp_send.at[number, YN + k],
                    recv_sem=disp_recv.at[number, k],
                    device_id=column(k),
                    device_id_type=MESH,
                )
                for k in range(1, YN)
            ]

        stays = last if step > 0 else 0

        @pl.when(section != stays)
        def _():
            for copy in copies(section + step):
                copy.start()

        @pl.when(section == edge)
        def _():
            for copy in own():
                copy.start()
            pltpu.make_async_copy(slab.at[n, y], buffer.at[place], disp_recv.at[number, 0]).start()

        def finish():
            @pl.when(section != stays)
            def _():
                for copy in copies(section + step):
                    copy.wait_send()

            @pl.when(section == edge)
            def _():
                for copy in own():
                    copy.wait_send()

        return finish

    def place_of(k):
        other = (y + YN - k) % YN
        return other % 2 * 2 + other // 2

    def spread_wait(number, buffer):
        for k in range(YN):
            arrive(buffer.at[place_of(k)], disp_recv.at[number, k])

    spread(0, lambda k: aux_in, aux)
    fwd_finish = shifted(1, 0, xf, 1, 0)
    spread(2, lambda k: slab.at[1, (y + k) % YN], xb)

    locals_ = []
    for i in range(items):
        for part, (src, dst) in enumerate(zip(own_refs(i), parts(i, x))):
            copy = pltpu.make_async_copy(src, dst, wloc.at[i, part])
            copy.start()
            locals_.append((i, copy))

    cut(2)
    grad_finish = shifted(3, 2, xg, -1, last)

    direct_wait(0)
    relay(0)
    own_send(2)

    spread_wait(0, aux)
    fwd_first = [aux[q, :, 0:1] < 0.5 for q in range(YN)]
    bwd_first = [aux[q, :, 2:3] < 0.5 for q in range(YN)]

    def divide(block, first, target):
        zero = jnp.zeros_like(block)
        target[:, pl.ds(0, full)] = jnp.where(first, block, zero)
        target[:, pl.ds(full, full)] = jnp.where(first, zero, block)

    spread_wait(1, xf)
    for q in range(YN):
        divide(xf[q], fwd_first[q], xcat.at[q // 2, 0, q % 2])
    spread_wait(2, xb)
    for q in range(YN):
        divide(xb[q], bwd_first[q], xcat.at[q // 2, 1, q % 2])

    def gather_send(i, ref):
        for k in (2, 1, 3):
            sent(ref, ref, ag_send.at[i, k - 1], ag_recv.at[i, k - 1], column(k))

    def gather_wait(i, buffer):
        for k in range(1, YN):
            arrive(buffer.at[place_of(k)], ag_recv.at[i, k - 1])

    def first_stage(i):
        if i < ng:
            mats = gu[i][...].reshape(XN * width, 2 * gates[i].size)
            source, out, into, keep, count = xcat, s1_out[i], s1_in[i], kept[i], 4
        else:
            d = i - ng
            mats = dn[d][...].reshape(XN * width, downs[d].size)
            source, out, into, keep, count = gcat, s1d_out[d], s1d_in[d], keptd[d], 2
        rows = source.at[1 - parity][...].reshape(count * tokens, 2 * full)
        given = jnp.dot(rows, mats, preferred_element_type=jnp.float32)
        out[...] = given.astype(jnp.bfloat16).reshape(out.shape)
        sent(out, into, s_send.at[i, 0], s_recv.at[i, 0], near)
        rows = source.at[parity][...].reshape(count * tokens, 2 * full)
        own = jnp.dot(rows, mats, preferred_element_type=jnp.float32)
        keep[...] = own.reshape(keep.shape)

    def second_stage(i):
        if i < ng:
            arrive(s1_in[i], s_recv.at[i, 0])
            for b in range(2):
                total = kept[i][b, 1 - high] + s1_in[i][b, 1 - high].astype(jnp.float32)
                s2_out[i][b] = total.astype(jnp.bfloat16)
            sent(s2_out[i], s2_in[i], s_send.at[i, 1], s_recv.at[i, 1], far)
        else:
            d = i - ng
            arrive(s1d_in[d], s_recv.at[i, 0])
            total = keptd[d][1 - high] + s1d_in[d][1 - high].astype(jnp.float32)
            s2d_out[d][...] = total.astype(jnp.bfloat16)
            sent(s2d_out[d], s2d_in[d], s_send.at[i, 1], s_recv.at[i, 1], far)

    def third_stage(i):
        if i < ng:
            c = gates[i].size
            arrive(s2_in[i], s_recv.at[i, 1])
            sums = [
                kept[i][b, high]
                + s1_in[i][b, high].astype(jnp.float32)
                + s2_in[i][b].astype(jnp.float32)
                for b in range(2)
            ]
            back[i][...] = sums[1]
            gate, up = sums[0][:, :c], sums[0][:, c:]
            hid[i][place] = (gate * jax.nn.sigmoid(gate) * up).astype(jnp.bfloat16)
            gather_send(i, hid[i].at[place])
        else:
            d = i - ng
            c, home = downs[d].size, downs[d].parent
            at = downs[d].start - gates[home].start
            arrive(s2d_in[d], s_recv.at[i, 1])
            grad_hidden = (
                keptd[d][high]
                + s1d_in[d][high].astype(jnp.float32)
                + s2d_in[d][...].astype(jnp.float32)
            )
            gate = back[home][:, at : at + c]
            up = back[home][:, gates[home].size + at : gates[home].size + at + c]
            sig = jax.nn.sigmoid(gate)
            grad_gate = grad_hidden * up * sig * (1.0 + gate * (1.0 - sig))
            grad_up = grad_hidden * (gate * sig)
            grads[d][place, :, pl.ds(0, c)] = grad_gate.astype(jnp.bfloat16)
            grads[d][place, :, pl.ds(c, c)] = grad_up.astype(jnp.bfloat16)
            gather_send(i, grads[d].at[place])

    def accumulate(values, first, mats, acc, start):
        zero = jnp.zeros_like(values[0])
        zeroth = jnp.concatenate([jnp.where(m, v, zero) for m, v in zip(first, values)], axis=0)
        other = jnp.concatenate([jnp.where(m, zero, v) for m, v in zip(first, values)], axis=0)
        total = lax.dot_general(zeroth, mats[:full], NT, preferred_element_type=jnp.float32)
        total += lax.dot_general(other, mats[full:], NT, preferred_element_type=jnp.float32)
        if start:
            acc[...] = total
        else:
            acc[...] += total

    def forward_sum(d):
        c, home = downs[d].size, downs[d].parent
        at = downs[d].start - gates[home].start
        if at == 0:
            gather_wait(home, hid[home])
        mats = dn[d][...].reshape(XN * width, c)
        values = [hid[home][q, :, at : at + c] for q in range(YN)]
        accumulate(values, fwd_first, mats, out_acc, d == 0)

    def backward_sum(d):
        c, home = downs[d].size, downs[d].parent
        at, size = downs[d].start - gates[home].start, gates[home].size
        gather_wait(ng + d, grads[d])
        mats = gu[home][...].reshape(XN * width, 2 * size)
        if c != size:
            mats = jnp.concatenate([mats[:, at : at + c], mats[:, size + at : size + at + c]], axis=1)
        accumulate([grads[d][q] for q in range(YN)], bwd_first, mats, grad_acc, d == 0)

    pieces = 2
    span = tokens // pieces

    def finished(number, q, residual, acc, where_lane):
        produced = acc[pl.ds(q * tokens, tokens), :].astype(jnp.bfloat16).astype(jnp.float32)
        weight = aux[q, :, where_lane : where_lane + 1]
        return (residual[q].astype(jnp.float32) + weight * produced).astype(jnp.bfloat16)

    def give(number, residual, acc, where_lane):
        for q in range(YN):
            ret_out[number, q] = finished(number, q, residual, acc, where_lane)

    def give_send(number, piece):
        rows = pl.ds(piece * span, span)
        for k in (2, 1, 3):
            other = (y + k) % YN
            sent(
                ret_out.at[number, other % 2 * 2 + other // 2, rows],
                ret_in.at[number, y, rows],
                ret_send.at[number, piece, k],
                ret_recv.at[number, piece, k],
                column(k),
            )

    def give_own(number):
        ret_in[number, y] = ret_out[number, place]

    stores = []

    def collect(number, result):
        for piece in range(pieces):
            rows = pl.ds(piece * span, span)
            for k in range(1, YN):
                other = (y + YN - k) % YN
                arrive(ret_in.at[number, other, rows], ret_recv.at[number, piece, k])
        whole[number] = jnp.concatenate(
            [ret_in[number, t, :, h * width : (h + 1) * width] for h in range(2) for t in range(YN)],
            axis=1,
        )
        stores.append(pltpu.make_async_copy(whole.at[number], result, store.at[number]))
        stores[-1].start()

    for i in range(items):
        d = i - ng
        if i + 1 < items:
            direct_wait(i + 1)
            relay(i + 1)
            own_send(i + 3)
        relay_wait(i)
        for number, copy in locals_:
            if number == i:
                copy.wait()
        if i == ng:
            spread_wait(3, xg)
            for q in range(YN):
                divide(xg[q], bwd_first[q], gcat.at[q // 2, q % 2])
        first_stage(i)
        if i > 0:
            third_stage(i - 1)
        if d >= 1:
            forward_sum(d - 1)
        if d == nd - 1:
            forward_sum(d)
            give(0, xf, out_acc, 1)
        second_stage(i)
        if d >= 2:
            backward_sum(d - 2)

    give_send(0, 0)
    give_own(0)
    if nd >= 2:
        backward_sum(nd - 2)
    third_stage(items - 1)
    give_send(0, 1)
    backward_sum(nd - 1)
    give(1, xg, grad_acc, 3)
    give_send(1, 0)
    give_send(1, 1)
    give_own(1)
    collect(0, fwd_out)
    fwd_finish()
    grad_finish()
    for copy in ending:
        copy.wait_send()
    collect(1, bwd_out)
    for copy in stores:
        copy.wait()


def fused(arrays, sections):
    tokens, model = arrays[0].shape
    width, units = arrays[3].shape
    gates, downs = chunks_of(units)
    full = model // YN
    bf16, f32 = jnp.bfloat16, jnp.float32
    dma = pltpu.SemaphoreType.DMA
    items = len(gates) + len(downs)
    whole = jax.ShapeDtypeStruct((tokens, model), bf16)
    ups = [2 * c.size for c in gates]
    sizes = [c.size for c in downs]

    def each(lead, tail, counts, kind):
        return [pltpu.VMEM(lead + (n,) + tail, kind) for n in counts]

    scratch = []
    scratch += each((XN, width), (), ups, bf16)
    scratch += each((2, 2, tokens), (), ups, bf16)
    scratch += each((2, 2, tokens), (), ups, bf16)
    scratch += each((2, tokens), (), ups, bf16)
    scratch += each((2, tokens), (), ups, bf16)
    scratch += each((2, 2, tokens), (), ups, f32)
    scratch += each((YN, tokens), (), [n // 2 for n in ups], bf16)
    scratch += each((tokens,), (), ups, f32)
    scratch += each((XN, width), (), sizes, bf16)
    scratch += each((2, tokens), (), sizes, bf16)
    scratch += each((2, tokens), (), sizes, bf16)
    scratch += each((tokens,), (), sizes, bf16)
    scratch += each((tokens,), (), sizes, bf16)
    scratch += each((2, tokens), (), sizes, f32)
    scratch += each((YN, tokens), (), [2 * n for n in sizes], bf16)
    scratch += [
        pltpu.VMEM((3, tokens, model), bf16),
        pltpu.VMEM((4, 1, tokens), f32),
        pltpu.VMEM((3, YN, tokens, full), bf16),
        pltpu.VMEM((tokens, 128), f32),
        pltpu.VMEM((YN, tokens, 128), f32),
        pltpu.VMEM((3, YN, tokens, full), bf16),
        pltpu.VMEM((2, 2, 2, tokens, 2 * full), bf16),
        pltpu.VMEM((2, 2, tokens, 2 * full), bf16),
        pltpu.VMEM((YN * tokens, full), f32),
        pltpu.VMEM((YN * tokens, full), f32),
        pltpu.VMEM((2, YN, tokens, full), bf16),
        pltpu.VMEM((2, YN, tokens, full), bf16),
        dma((7,)),
        dma((items, 2, 2)),
        dma((items, 2, 2)),
        dma((items, 2)),
        dma((items, 2)),
        dma((items, 2)),
        dma((4, 2 * YN)),
        dma((4, YN)),
        dma((items, 2)),
        dma((items, 2)),
        dma((items, YN - 1)),
        dma((items, YN - 1)),
        dma((2, 2, YN)),
        dma((2, 2, YN)),
        dma((2,)),
    ]
    return pl.pallas_call(
        functools.partial(kernel, sections, gates, downs),
        out_shape=(whole, whole),
        in_specs=[pl.BlockSpec(memory_space=pl.ANY)] * 10,
        out_specs=(pl.BlockSpec(memory_space=pl.ANY),) * 2,
        scratch_shapes=scratch,
        compiler_params=pltpu.CompilerParams(
            collective_id=0, has_side_effects=True, vmem_limit_bytes=62 * 1024 * 1024
        ),
    )(*arrays)


def body(sections, fwd_in, bwd_in, bwd_grad_in, w_gate, w_up, w_down, fwd_ids, fwd_gates, bwd_ids, bwd_gates):
    def line(values):
        return values.astype(jnp.float32).reshape(1, -1)

    arrays = [fwd_in[0], bwd_in[0], bwd_grad_in[0], w_gate[0], w_up[0], w_down[0].T]
    arrays += [line(fwd_ids), line(fwd_gates), line(bwd_ids), line(bwd_gates)]
    fwd, bwd = fused(arrays, sections)
    return fwd[None], bwd[None]


def solution(mesh):
    rows = P("pipe", "expert", None)
    return jax.shard_map(
        functools.partial(body, mesh.shape["pipe"]),
        mesh=mesh,
        in_specs=(rows, rows, rows, rows, rows, P("pipe", None, "expert"), rows, rows, rows, rows),
        out_specs=(rows, rows),
        check_vma=False,
    )
```

time: 167 us -> 154 us (0.922)
  the two profiles are of different devices: /device:TPU:250 before, /device:TPU:132 now
where the time goes in v2:
time: 154 us
  Pallas kernels  149 us (97%)
  local copies, waits for them, and re-layouts  3.3 us (2%)
    pallas_call x1, Pallas kernels, fused(): pl.pallas_call(functools.partial(kernel, sections, gates, downs), out_sha...  149 us
    unnamed x8, local copies, waits for them, and re-layouts  3.3 us

profile of v2, /device:TPU:132, one launch (start us, length us, event | category | flops | bytes accessed | tf_op | source)
XLA Modules:
  0.0 153.8 jit_solution(2204368388055180771)
XLA Ops:
  0.6 0.0 copy-start.1
  0.6 0.0 copy-start.2
  0.6 0.6 copy-done.1
  1.3 0.0 copy-done.2
  1.3 0.5 convert_bitcast_fusion
  1.8 149.3 %shard_map.113 = (bf16[64,3584]{1,0:T(8,128)(2,1)}, bf16[64,3584]{1,0:T(8,128)(2,1)}) custom-call(bf16[64,3584]{1,0:T(8,128)(2,1)} %bitcast.19, bf16[64,3584]{1,0:T(8,128)(2,1)} %bitcast.20, bf16[64,3584]{1,0:T(8,128)(2,1)} %bitcast.21, bf16[448,1024]{1,0:T(8,128)(2,1)} %bitcast.16, bf16[448,1024]{1,0:T(8,128)(2,1)} %bitcast.17, bf16[448,1024]{1,0:T(8,128)(2,1)} %bitcast.18, ...), custom_call_target="tpu_custom_call" | custom-call | tf_op jit(solution)/shard_map/pallas_call | solution.py:553
  151.2 0.0 copy-start
  151.2 1.9 %copy.14 = bf16[1,64,3584]{2,1,0:T(8,128)(2,1)} copy(bf16[1,64,3584]{2,1,0:T(8,128)(2,1)} %bitcast.23) | data formatting | bytes 917504
  153.1 0.0 copy-done
  153.1 0.8 copy.15
Async XLA Ops:
  0.6 0.7 copy-start.1
  0.6 0.7 copy-start.2
  151.2 1.9 %copy-start = (bf16[64,3584]{1,0:T(8,128)(2,1)S(1)}, bf16[64,3584]{1,0:T(8,128)(2,1)}, u32[]{:S(2)}) copy-start(bf16[64,3584]{1,0:T(8,128)(2,1)} %get-tuple-element.5) | copy-start | bytes 1376260

commit v3 on v2

--- a/solution.py
+++ b/solution.py
@@ -48,7 +48,7 @@
     ng, nd = len(gates), len(downs)
     gu, s1_out, s1_in, s2_out, s2_in, kept, hid, back = [take(ng) for _ in range(8)]
     dn, s1d_out, s1d_in, s2d_out, s2d_in, keptd, grads = [take(nd) for _ in range(7)]
-    (whole, small, slab, aux_in, aux, land, xcat, gcat) = take(8)
+    (whole, ids, weights, slab, aux_in, aux, land, xcat, gcat) = take(9)
     (out_acc, grad_acc, ret_out, ret_in) = take(4)
     (load, wdir_send, wdir_recv, wrel_send, wrel_recv, wloc) = take(6)
     (disp_send, disp_recv, s_send, s_recv, ag_send, ag_recv, ret_send, ret_recv, store) = take(9)
@@ -58,9 +58,11 @@
     me = lax.axis_index("expert")
     x = me // YN
     y = me % YN
-    parity = y % 2
-    high = y // 2
-    place = parity * 2 + high
+    place = y
+    half = y // 2
+    rest = 1 - half
+    inner = (y == 1) | (y == 2)
+    outer = (y == 0) | (y == 3)
     tokens = fwd_in.shape[0]
     width = w_gate.shape[0]
     half_rows = width // 2
@@ -70,7 +72,8 @@
     loads = []
     for n, (src, dst) in enumerate(
         [(fwd_in, whole.at[0]), (bwd_in, whole.at[1]), (grad_in, whole.at[2])]
-        + [(ref, small.at[j]) for j, ref in enumerate((fwd_ids, fwd_gates, bwd_ids, bwd_gates))]
+        + [(fwd_ids, ids.at[0]), (fwd_gates, weights.at[0])]
+        + [(bwd_ids, ids.at[1]), (bwd_gates, weights.at[1])]
     ):
         loads.append(pltpu.make_async_copy(src, dst, load.at[n]))
         loads[-1].start()
@@ -81,8 +84,10 @@
     def row(k):
         return (section, (x + k) % XN * YN + y)
 
-    near = (section, x * YN + y + 1 - 2 * parity)
-    far = (section, x * YN + (y + 2) % YN)
+    my_inner = (section, x * YN + 1 + half)
+    my_outer = (section, x * YN + 3 * half)
+    far_outer = (section, x * YN + 3 - 3 * half)
+    across = (section, x * YN + 2 - half)
 
     barrier = pltpu.get_barrier_semaphore()
 
@@ -123,20 +128,21 @@
     lane = lax.broadcasted_iota(jnp.int32, (tokens, 128), 1)
     table = jnp.zeros((tokens, 128), jnp.float32)
     for j in range(4):
-        line = jnp.broadcast_to(small[j], (tokens, tokens))
+        line = (weights if j % 2 else ids)[j // 2].astype(jnp.float32)
+        line = jnp.broadcast_to(line, (tokens, tokens))
         stood = jnp.sum(jnp.where(eye, line, 0.0), axis=1, keepdims=True)
         table = jnp.where(lane == j, stood, table)
     aux_in[...] = table
     cut(0)
     cut(1)
 
-    inner = jnp.where(section < last, YN, 0) + jnp.where(section > 0, YN, 0)
-    pl.semaphore_wait(barrier, YN + 1 + inner)
-
-    ending = []
-
-    def send(src, dst, send_sem, recv_sem, device):
-        copy = pltpu.make_async_remote_copy(
+    others = jnp.where(section < last, YN, 0) + jnp.where(section > 0, YN, 0)
+    pl.semaphore_wait(barrier, YN + 1 + others)
+
+    ending, inner_ending, outer_ending = [], [], []
+
+    def remote(src, dst, send_sem, recv_sem, device):
+        return pltpu.make_async_remote_copy(
             src_ref=src,
             dst_ref=dst,
             send_sem=send_sem,
@@ -144,11 +150,15 @@
             device_id=device,
             device_id_type=MESH,
         )
+
+    def sent(*args):
+        copy = remote(*args)
         copy.start()
-        return copy
-
-    def sent(*args):
-        ending.append(send(*args))
+        ending.append(copy)
+
+    def sent_by(end, args):
+        remote(*args()).start()
+        end.append(args)
 
     def arrive(dst, sem):
         pltpu.make_async_copy(dst, dst, sem).wait()
@@ -260,8 +270,7 @@
         return finish
 
     def place_of(k):
-        other = (y + YN - k) % YN
-        return other % 2 * 2 + other // 2
+        return (y + YN - k) % YN
 
     def spread_wait(number, buffer):
         for k in range(YN):
@@ -301,76 +310,105 @@
     for q in range(YN):
         divide(xb[q], bwd_first[q], xcat.at[q // 2, 1, q % 2])
 
-    def gather_send(i, ref):
-        for k in (2, 1, 3):
-            sent(ref, ref, ag_send.at[i, k - 1], ag_recv.at[i, k - 1], column(k))
-
-    def gather_wait(i, buffer):
-        for k in range(1, YN):
-            arrive(buffer.at[place_of(k)], ag_recv.at[i, k - 1])
+    def gather_buffer(i):
+        return hid[i] if i < ng else grads[i - ng]
+
+    def gather_args(i, part, n, device):
+        ref = gather_buffer(i).at[part]
+        return ref, ref, ag_send.at[i, n], ag_recv.at[i, n], device
+
+    def gather_send(i):
+        targets = [across, my_outer] + ([far_outer] if i == items - 1 else [])
+        for n, device in enumerate(targets):
+            sent_by(inner_ending, functools.partial(gather_args, i, half, n, device))
+
+    def gather_relay(i):
+        @pl.when(inner)
+        def _():
+            arrive(gather_buffer(i).at[rest], ag_recv.at[i, 0])
+            if i < items - 1:
+                sent_by(inner_ending, functools.partial(gather_args, i, rest, 2, my_outer))
+
+    def gather_wait(i):
+        buffer = gather_buffer(i)
+
+        @pl.when(outer)
+        def _():
+            arrive(buffer.at[half], ag_recv.at[i, 1])
+            arrive(buffer.at[rest], ag_recv.at[i, 2])
+
+    def stage_refs(i):
+        if i < ng:
+            return s1_out[i], s1_in[i], s2_out[i], s2_in[i], kept[i]
+        d = i - ng
+        return s1d_out[d], s1d_in[d], s2d_out[d], s2d_in[d], keptd[d]
+
+    def near_args(i, n):
+        out, into, _, _, _ = stage_refs(i)
+        return out.at[n], into.at[n], s_send.at[i, n], s_recv.at[i, n], my_inner
+
+    def across_args(i):
+        _, _, out, across_in, _ = stage_refs(i)
+        return out, across_in, s_send.at[i, 2], s_recv.at[i, 2], across
 
     def first_stage(i):
         if i < ng:
             mats = gu[i][...].reshape(XN * width, 2 * gates[i].size)
-            source, out, into, keep, count = xcat, s1_out[i], s1_in[i], kept[i], 4
+            source, count = xcat, 4
         else:
-            d = i - ng
-            mats = dn[d][...].reshape(XN * width, downs[d].size)
-            source, out, into, keep, count = gcat, s1d_out[d], s1d_in[d], keptd[d], 2
-        rows = source.at[1 - parity][...].reshape(count * tokens, 2 * full)
-        given = jnp.dot(rows, mats, preferred_element_type=jnp.float32)
-        out[...] = given.astype(jnp.bfloat16).reshape(out.shape)
-        sent(out, into, s_send.at[i, 0], s_recv.at[i, 0], near)
-        rows = source.at[parity][...].reshape(count * tokens, 2 * full)
-        own = jnp.dot(rows, mats, preferred_element_type=jnp.float32)
-        keep[...] = own.reshape(keep.shape)
+            mats = dn[i - ng][...].reshape(XN * width, downs[i - ng].size)
+            source, count = gcat, 2
+        out, into, _, _, keep = stage_refs(i)
+        for n, owner in enumerate((rest, half)):
+            rows = source.at[owner][...].reshape(count * tokens, 2 * full)
+            partial_sum = jnp.dot(rows, mats, preferred_element_type=jnp.float32)
+            keep[n] = partial_sum.reshape(keep.shape[1:])
+
+            @pl.when(outer)
+            def _():
+                out[n] = keep[n].astype(jnp.bfloat16)
+                sent_by(outer_ending, functools.partial(near_args, i, n))
 
     def second_stage(i):
-        if i < ng:
-            arrive(s1_in[i], s_recv.at[i, 0])
-            for b in range(2):
-                total = kept[i][b, 1 - high] + s1_in[i][b, 1 - high].astype(jnp.float32)
-                s2_out[i][b] = total.astype(jnp.bfloat16)
-            sent(s2_out[i], s2_in[i], s_send.at[i, 1], s_recv.at[i, 1], far)
-        else:
-            d = i - ng
-            arrive(s1d_in[d], s_recv.at[i, 0])
-            total = keptd[d][1 - high] + s1d_in[d][1 - high].astype(jnp.float32)
-            s2d_out[d][...] = total.astype(jnp.bfloat16)
-            sent(s2d_out[d], s2d_in[d], s_send.at[i, 1], s_recv.at[i, 1], far)
+        _, into, out, across_in, keep = stage_refs(i)
+
+        @pl.when(inner)
+        def _():
+            arrive(into.at[0], s_recv.at[i, 0])
+            out[...] = (keep[0] + into[0].astype(jnp.float32)).astype(jnp.bfloat16)
+            sent_by(inner_ending, functools.partial(across_args, i))
 
     def third_stage(i):
-        if i < ng:
-            c = gates[i].size
-            arrive(s2_in[i], s_recv.at[i, 1])
-            sums = [
-                kept[i][b, high]
-                + s1_in[i][b, high].astype(jnp.float32)
-                + s2_in[i][b].astype(jnp.float32)
-                for b in range(2)
-            ]
-            back[i][...] = sums[1]
-            gate, up = sums[0][:, :c], sums[0][:, c:]
-            hid[i][place] = (gate * jax.nn.sigmoid(gate) * up).astype(jnp.bfloat16)
-            gather_send(i, hid[i].at[place])
-        else:
-            d = i - ng
-            c, home = downs[d].size, downs[d].parent
-            at = downs[d].start - gates[home].start
-            arrive(s2d_in[d], s_recv.at[i, 1])
-            grad_hidden = (
-                keptd[d][high]
-                + s1d_in[d][high].astype(jnp.float32)
-                + s2d_in[d][...].astype(jnp.float32)
-            )
-            gate = back[home][:, at : at + c]
-            up = back[home][:, gates[home].size + at : gates[home].size + at + c]
-            sig = jax.nn.sigmoid(gate)
-            grad_gate = grad_hidden * up * sig * (1.0 + gate * (1.0 - sig))
-            grad_up = grad_hidden * (gate * sig)
-            grads[d][place, :, pl.ds(0, c)] = grad_gate.astype(jnp.bfloat16)
-            grads[d][place, :, pl.ds(c, c)] = grad_up.astype(jnp.bfloat16)
-            gather_send(i, grads[d].at[place])
+        _, into, _, across_in, keep = stage_refs(i)
+
+        @pl.when(inner)
+        def _():
+            arrive(into.at[1], s_recv.at[i, 1])
+            arrive(across_in, s_recv.at[i, 2])
+            if i < ng:
+                c = gates[i].size
+                sums = [
+                    keep[1, b] + into[1, b].astype(jnp.float32) + across_in[b].astype(jnp.float32)
+                    for b in range(2)
+                ]
+                back[i][...] = sums[1]
+                gate, up = sums[0][:, :c], sums[0][:, c:]
+                hid[i][half] = (gate * jax.nn.sigmoid(gate) * up).astype(jnp.bfloat16)
+            else:
+                d = i - ng
+                c, home = downs[d].size, downs[d].parent
+                at = downs[d].start - gates[home].start
+                grad_hidden = (
+                    keep[1] + into[1].astype(jnp.float32) + across_in[...].astype(jnp.float32)
+                )
+                gate = back[home][:, at : at + c]
+                up = back[home][:, gates[home].size + at : gates[home].size + at + c]
+                sig = jax.nn.sigmoid(gate)
+                grad_gate = grad_hidden * up * sig * (1.0 + gate * (1.0 - sig))
+                grad_up = grad_hidden * (gate * sig)
+                grads[d][half, :, pl.ds(0, c)] = grad_gate.astype(jnp.bfloat16)
+                grads[d][half, :, pl.ds(c, c)] = grad_up.astype(jnp.bfloat16)
+            gather_send(i)
 
     def accumulate(values, first, mats, acc, start):
         zero = jnp.zeros_like(values[0])
@@ -383,23 +421,28 @@
         else:
             acc[...] += total
 
+    def rows_of(buffer, at, c):
+        return [
+            buffer[q // 2, q % 2 * tokens : (q % 2 + 1) * tokens, at : at + c] for q in range(YN)
+        ]
+
     def forward_sum(d):
         c, home = downs[d].size, downs[d].parent
         at = downs[d].start - gates[home].start
         if at == 0:
-            gather_wait(home, hid[home])
+            gather_wait(home)
         mats = dn[d][...].reshape(XN * width, c)
-        values = [hid[home][q, :, at : at + c] for q in range(YN)]
+        values = rows_of(hid[home], at, c)
         accumulate(values, fwd_first, mats, out_acc, d == 0)
 
     def backward_sum(d):
         c, home = downs[d].size, downs[d].parent
         at, size = downs[d].start - gates[home].start, gates[home].size
-        gather_wait(ng + d, grads[d])
+        gather_wait(ng + d)
         mats = gu[home][...].reshape(XN * width, 2 * size)
         if c != size:
             mats = jnp.concatenate([mats[:, at : at + c], mats[:, size + at : size + at + c]], axis=1)
-        accumulate([grads[d][q] for q in range(YN)], bwd_first, mats, grad_acc, d == 0)
+        accumulate(rows_of(grads[d], 0, 2 * c), bwd_first, mats, grad_acc, d == 0)
 
     pieces = 2
     span = tokens // pieces
@@ -418,7 +461,7 @@
         for k in (2, 1, 3):
             other = (y + k) % YN
             sent(
-                ret_out.at[number, other % 2 * 2 + other // 2, rows],
+                ret_out.at[number, other, rows],
                 ret_in.at[number, y, rows],
                 ret_send.at[number, piece, k],
                 ret_recv.at[number, piece, k],
@@ -466,15 +509,19 @@
             forward_sum(d)
             give(0, xf, out_acc, 1)
         second_stage(i)
+        if i > 0:
+            gather_relay(i - 1)
+        if i == items - 1:
+            give_send(0, 0)
+            give_own(0)
         if d >= 2:
             backward_sum(d - 2)
 
-    give_send(0, 0)
-    give_own(0)
     if nd >= 2:
         backward_sum(nd - 2)
     third_stage(items - 1)
     give_send(0, 1)
+    gather_relay(items - 1)
     backward_sum(nd - 1)
     give(1, xg, grad_acc, 3)
     give_send(1, 0)
@@ -485,6 +532,17 @@
     grad_finish()
     for copy in ending:
         copy.wait_send()
+
+    @pl.when(inner)
+    def _():
+        for args in inner_ending:
+            remote(*args()).wait_send()
+
+    @pl.when(outer)
+    def _():
+        for args in outer_ending:
+            remote(*args()).wait_send()
+
     collect(1, bwd_out)
     for copy in stores:
         copy.wait()
@@ -507,23 +565,24 @@
 
     scratch = []
     scratch += each((XN, width), (), ups, bf16)
-    scratch += each((2, 2, tokens), (), ups, bf16)
-    scratch += each((2, 2, tokens), (), ups, bf16)
-    scratch += each((2, tokens), (), ups, bf16)
-    scratch += each((2, tokens), (), ups, bf16)
-    scratch += each((2, 2, tokens), (), ups, f32)
-    scratch += each((YN, tokens), (), [n // 2 for n in ups], bf16)
-    scratch += each((tokens,), (), ups, f32)
+    scratch += each((2, 2, 2 * tokens), (), ups, bf16)
+    scratch += each((2, 2, 2 * tokens), (), ups, bf16)
+    scratch += each((2, 2 * tokens), (), ups, bf16)
+    scratch += each((2, 2 * tokens), (), ups, bf16)
+    scratch += each((2, 2, 2 * tokens), (), ups, f32)
+    scratch += each((2, 2 * tokens), (), [n // 2 for n in ups], bf16)
+    scratch += each((2 * tokens,), (), ups, f32)
     scratch += each((XN, width), (), sizes, bf16)
-    scratch += each((2, tokens), (), sizes, bf16)
-    scratch += each((2, tokens), (), sizes, bf16)
-    scratch += each((tokens,), (), sizes, bf16)
-    scratch += each((tokens,), (), sizes, bf16)
-    scratch += each((2, tokens), (), sizes, f32)
-    scratch += each((YN, tokens), (), [2 * n for n in sizes], bf16)
+    scratch += each((2, 2 * tokens), (), sizes, bf16)
+    scratch += each((2, 2 * tokens), (), sizes, bf16)
+    scratch += each((2 * tokens,), (), sizes, bf16)
+    scratch += each((2 * tokens,), (), sizes, bf16)
+    scratch += each((2, 2 * tokens), (), sizes, f32)
+    scratch += each((2, 2 * tokens), (), [2 * n for n in sizes], bf16)
     scratch += [
         pltpu.VMEM((3, tokens, model), bf16),
-        pltpu.VMEM((4, 1, tokens), f32),
+        pltpu.VMEM((2, 1, tokens), jnp.int32),
+        pltpu.VMEM((2, 1, tokens), f32),
         pltpu.VMEM((3, YN, tokens, full), bf16),
         pltpu.VMEM((tokens, 128), f32),
         pltpu.VMEM((YN, tokens, 128), f32),
@@ -542,8 +601,8 @@
         dma((items, 2)),
         dma((4, 2 * YN)),
         dma((4, YN)),
-        dma((items, 2)),
-        dma((items, 2)),
+        dma((items, 3)),
+        dma((items, 3)),
         dma((items, YN - 1)),
         dma((items, YN - 1)),
         dma((2, 2, YN)),
@@ -564,7 +623,7 @@
 
 def body(sections, fwd_in, bwd_in, bwd_grad_in, w_gate, w_up, w_down, fwd_ids, fwd_gates, bwd_ids, bwd_gates):
     def line(values):
-        return values.astype(jnp.float32).reshape(1, -1)
+        return values.reshape(1, -1)
 
     arrays = [fwd_in[0], bwd_in[0], bwd_grad_in[0], w_gate[0], w_up[0], w_down[0].T]
     arrays += [line(fwd_ids), line(fwd_gates), line(bwd_ids), line(bwd_gates)]

time: 154 us -> 145 us (0.942)
  the two profiles are of different devices: /device:TPU:132 before, /device:TPU:56 now
where the time goes in v3:
time: 145 us; the launch traced here: 144 us
  Pallas kernels  141 us (97%)
  local copies, waits for them, and re-layouts  2.64 us (2%)
    pallas_call x1, Pallas kernels, fused(): pl.pallas_call(functools.partial(kernel, sections, gates, downs), out_sha...  141 us

profile of v3, /device:TPU:56, one launch (start us, length us, event | category | flops | bytes accessed | tf_op | source)
XLA Modules:
  0.0 144.4 jit_solution(9604528392084276874)
XLA Ops:
  0.6 141.1 %shard_map.113 = (bf16[64,3584]{1,0:T(8,128)(2,1)}, bf16[64,3584]{1,0:T(8,128)(2,1)}) custom-call(bf16[64,3584]{1,0:T(8,128)(2,1)} %bitcast.17, bf16[64,3584]{1,0:T(8,128)(2,1)} %bitcast.18, bf16[64,3584]{1,0:T(8,128)(2,1)} %bitcast.19, bf16[448,1024]{1,0:T(8,128)(2,1)} %bitcast.14, bf16[448,1024]{1,0:T(8,128)(2,1)} %bitcast.15, bf16[448,1024]{1,0:T(8,128)(2,1)} %bitcast.16, ...), custom_call_target="tpu_custom_call" | custom-call | tf_op jit(solution)/shard_map/pallas_call | solution.py:612
  141.8 0.0 copy-start
  141.8 1.9 %copy.14 = bf16[1,64,3584]{2,1,0:T(8,128)(2,1)} copy(bf16[1,64,3584]{2,1,0:T(8,128)(2,1)} %bitcast.21) | data formatting | bytes 917504
  143.6 0.0 copy-done
  143.6 0.8 copy.15
Async XLA Ops:
  141.8 1.9 %copy-start = (bf16[64,3584]{1,0:T(8,128)(2,1)S(1)}, bf16[64,3584]{1,0:T(8,128)(2,1)}, u32[]{:S(2)}) copy-start(bf16[64,3584]{1,0:T(8,128)(2,1)} %get-tuple-element.5) | copy-start | bytes 1376260
